TPU v7x, 128 devices: a whole 4x4x4 slice. The times are simulated.
128 devices in a mesh: zone: 4 (over y), block: 32 (over x, z, core).
Axes of the slice: x: 4, y: 4, z: 4, core: 2. Of those that a mesh axis runs over, the one named last changes fastest.
Arguments:
- start_state: float32 [5, 4, 4096, 512], P(None, 'zone', 'block'), may hold values from -6 to 6
- diffusivity: float32 [4, 4096, 512], P('zone', 'block'), may hold values from 0.02 to 0.2
- donor_map: int32 [4, 4, 4096], P(None, 'zone'), may hold values from 0 to 4095, as said below
- donor_weight: float32 [4, 4, 4096], P(None, 'zone'), may hold values from 0 to 1
- coupling: float32 [5, 5], replicated, may hold values from -0.15 to 0.15
- final_cotangent: float32 [5, 4, 4096, 512], P(None, 'zone', 'block'), may hold values from -6 to 6
- wall_area: float32 [4, 12288], P('zone', 'block'), may hold values from 0.5 to 2
- wall_projection: float32 [3, 5], replicated, may hold values from -2.5 to 2.5
- center_ids: int32 [4, 8, 12288], P('zone', None, 'block'), may hold values from 0 to 32767
- center_dist: float32 [4, 8, 12288], P('zone', None, 'block'), may hold values from 0 to 0.95
Outputs:
- adjoint_start: float32 [5, 4, 4096, 512], P(None, 'zone', 'block')
- shape_gradient: float32 [3, 32768], P(None, ('zone', 'block'))
Inputs may be any that keep to these rules, and one draw needn't show every extreme that they name: For each step n and zone z there is an offset t, and donor_map[n, z, a] = (a + t + e) mod 4096 with e in 0 to 4.
All inputs are finite; a program needn't handle non-finite values.
Results may differ from a plain program's by a relative error of at most 0.0003.
Values sent between devices are 32-bit elements; how exact they have to be, the bound alone decides.
A program may use at most 128 MiB of HBM per device.

v0:
```python
import jax
import jax.numpy as jnp
from jax import lax
from jax.sharding import PartitionSpec as P

CP_DEV = 256


def swapped(value, axis, bit):
    mask = 2**bit
    pairs = [(source, source ^ mask) for source in range(lax.axis_size(axis))]
    return lax.ppermute(value, axis, pairs)


def extended(x, sides, width):
    for axis, dim in sides:
        size, length = (lax.axis_size(axis), x.shape[dim])
        up = [(i, (i + 1) % size) for i in range(size)]
        down = [(j, i) for i, j in up]
        last = lax.slice_in_dim(x, length - width, length, axis=dim)
        leading = lax.slice_in_dim(x, 0, width, axis=dim)
        before = lax.ppermute(last, axis, up)
        after = lax.ppermute(leading, axis, down)
        x = jnp.concatenate([before, x, after], axis=dim)
    return x


def advance(
    current, kappa_rows, partner_face, donor_rows, donor_share, first_row, total_rows, coupling
):
    middle = current[:, :, 1:-1]
    row_count = middle.shape[2]
    global_rows = (first_row + jnp.arange(row_count, dtype=jnp.int32)) % total_rows
    first_donor = jnp.take(donor_rows, global_rows)
    donor_part = jnp.take(donor_share, global_rows)
    second_donor = (first_donor + 1) % total_rows
    ghost = donor_part * jnp.take(partner_face, first_donor, axis=1) + (
        1.0 - donor_part
    ) * jnp.take(partner_face, second_donor, axis=1)
    outward = jnp.concatenate([middle[..., 1:], ghost[:, None, :, None]], axis=-1)
    inward = jnp.concatenate([jnp.zeros_like(middle[..., :1]), middle[..., :-1]], axis=-1)
    laplace = current[:, :, 2:] + current[:, :, :-2] + outward + inward - 4.0 * middle
    reaction = jnp.einsum(
        "vw,wzar->vzar", coupling, jnp.tanh(middle), precision=lax.Precision.HIGHEST
    )
    return middle + kappa_rows[:, :, 1:-1] * laplace - reaction


def gather_face(outer_face):
    mirrored = swapped(outer_face, "zone", 0)
    partner_face = lax.all_gather(mirrored, "block", axis=1, tiled=True)
    return partner_face


def return_face(ghost_adjoint, donor_rows, donor_share, own_global, total_rows):
    first_donor = jnp.take(donor_rows, own_global)
    donor_part = jnp.take(donor_share, own_global)
    second_donor = (first_donor + 1) % total_rows
    variables = ghost_adjoint.shape[0]
    collected = jnp.zeros((variables, total_rows), jnp.float32)
    collected = collected.at[:, first_donor].add(donor_part * ghost_adjoint)
    collected = collected.at[:, second_donor].add((1.0 - donor_part) * ghost_adjoint)
    partial_rows = lax.psum_scatter(collected, "block", scatter_dimension=1, tiled=True)
    owned = swapped(partial_rows, "zone", 0)
    return owned


def local(
    start_state,
    diffusivity,
    donor_map,
    donor_weight,
    coupling,
    final_cotangent,
    wall_area,
    wall_projection,
    center_ids,
    center_dist,
):
    variables, _, own_rows, radial = start_state.shape
    block_count = lax.axis_size("block")
    zone_count = lax.axis_size("zone")
    total_rows = own_rows * block_count
    block_index = lax.axis_index("block")
    step_count = donor_map.shape[0]
    kappa_own = diffusivity[None]
    stacked = jnp.concatenate([start_state, kappa_own], axis=0)
    rim_width = 1
    widened = extended(stacked, (("block", 2),), rim_width)
    kappa_wide = widened[variables:]
    current = widened[:variables]
    history = []
    for time_step in range(step_count - 1):
        margin = 1
        if time_step > 0:
            current = extended(current, (("block", 2),), 1)
        interior = current[:, :, margin : margin + own_rows]
        history.append(interior)
        partner_face = gather_face(interior[:, 0, :, radial - 1])
        current = advance(
            current,
            kappa_wide,
            partner_face,
            donor_map[time_step, 0],
            donor_weight[time_step, 0],
            block_index * own_rows - margin + 1,
            total_rows,
            coupling,
        )
    history.append(current)
    own_global = block_index * own_rows + jnp.arange(own_rows, dtype=jnp.int32)
    adjoint = final_cotangent
    wall_product = jnp.zeros((variables, own_rows), jnp.float32)
    for time_step in reversed(range(step_count)):
        state = history[time_step]
        wall_product = wall_product + adjoint[:, 0, :, 0] * state[:, 0, :, 0]
        scaled = kappa_own * adjoint
        scaled_wide = extended(scaled, (("block", 2),), 1)
        outward = jnp.concatenate([scaled[..., 1:], jnp.zeros_like(scaled[..., :1])], axis=-1)
        inward = jnp.concatenate([jnp.zeros_like(scaled[..., :1]), scaled[..., :-1]], axis=-1)
        transposed = (
            scaled_wide[:, :, 2:] + scaled_wide[:, :, :-2] + outward + inward - 4.0 * scaled
        )
        tangent = jnp.tanh(state)
        pulled = jnp.einsum("wv,wzar->vzar", coupling, adjoint, precision=lax.Precision.HIGHEST)
        face_back = return_face(
            scaled[:, 0, :, radial - 1],
            donor_map[time_step, 0],
            donor_weight[time_step, 0],
            own_global,
            total_rows,
        )
        adjoint = adjoint + transposed - (1.0 - tangent * tangent) * pulled
        adjoint = adjoint.at[:, 0, :, radial - 1].add(face_back)
    per_cell = wall_area.shape[1] // own_rows
    repeated = jnp.repeat(wall_product, per_cell, axis=1)
    sensitivity = wall_area * jnp.einsum(
        "cv,vw->cw", wall_projection, repeated, precision=lax.Precision.HIGHEST
    )
    distance = center_dist[0]
    kernel = (1.0 - distance) ** 4 * (4.0 * distance + 1.0)
    weighted = kernel[None] * sensitivity[:, None, :]
    point_total = CP_DEV * zone_count * block_count
    accumulated = (
        jnp.zeros((3, point_total), jnp.float32)
        .at[:, center_ids[0].reshape(-1)]
        .add(weighted.reshape(3, -1))
    )
    summed = lax.psum(accumulated, ("zone", "block"))
    owned_points = lax.dynamic_slice_in_dim(
        summed, lax.axis_index(("zone", "block")) * CP_DEV, CP_DEV, 1
    )
    return (adjoint, owned_points)


def solution(mesh):
    return jax.shard_map(
        local,
        mesh=mesh,
        in_specs=(
            P(None, "zone", "block", None),
            P("zone", "block", None),
            P(None, "zone", None),
            P(None, "zone", None),
            P(),
            P(None, "zone", "block", None),
            P("zone", "block"),
            P(),
            P("zone", None, "block"),
            P("zone", None, "block"),
        ),
        out_specs=(P(None, "zone", "block", None), P(None, ("zone", "block"))),
        check_vma=False,
    )
```

profile of v0, /device:TPU:1, one launch (start us, length us, event | category | flops | bytes accessed | tf_op | source)
XLA Modules:
  0.0 817.1 jit_solution(9083679854984549254)
XLA Ops:
  20.3 3.9 collective-permute-start
  33.6 2.8 scatter_custom_fusion
  36.4 4.4 scatter_fusion
  54.4 5.0 fusion.139
  59.4 2.8 fusion.134
  73.7 33.1 %all_gather.9 = f32[5,4096]{0,1:T(8,128)} all-gather(f32[5,128]{0,1:T(8,128)} %collective-permute-done.4), channel_id=1, replica_groups=mesh['zone'=4,'block'=32] {'block'}, dimensions={1}, use_global_device_ids=true | all-gather | bytes 84480 | tf_op jit(solution)/shard_map/all_gather | solution.py:51
  113.9 8.2 %fusion.40 = f32[5,1,128,512]{3,0,2,1:T(8,128)S(1)} fusion(f32[5,1,128,512]{3,0,2,1:T(8,128)} %copy-done.1, f32[6,1,1,512]{3,0,2,1:T(8,128)} %collective-permute-done.3, f32[1,1,128,512]{3,0,2,1:T(1,128)} %copy-done.10, f32[6,1,1,512]{3,0,2,1:T(8,128)} %collective-permute-done.2, f32[5,1,128,1]{3,0,2,1:T(8,128)} %copy.89, ...), kind=kOutput, calls=%fused_computation.80 | convolution fusion | flops 23920640 | bytes 5789284 | tf_op jit(solution)/shard_map/vw,wzar->vzar/dot_general | solution.py:43
  123.6 2.8 fusion.137
  132.8 28.6 %all_gather.10 = f32[5,4096]{0,1:T(8,128)} all-gather(f32[5,128]{0,1:T(8,128)S(1)} %collective-permute-done.7), channel_id=1, replica_groups=mesh['zone'=4,'block'=32] {'block'}, dimensions={1}, use_global_device_ids=true | all-gather | bytes 84480 | tf_op jit(solution)/shard_map/all_gather | solution.py:51
  168.6 8.2 fusion.33
  186.7 28.7 %all_gather.11 = f32[5,4096]{0,1:T(8,128)} all-gather(f32[5,128]{0,1:T(8,128)S(1)} %collective-permute-done.10), channel_id=1, replica_groups=mesh['zone'=4,'block'=32] {'block'}, dimensions={1}, use_global_device_ids=true | all-gather | bytes 84480 | tf_op jit(solution)/shard_map/all_gather | solution.py:51
  222.5 9.9 %fusion.26 = f32[5,1,128,512]{3,0,2,1:T(8,128)} fusion(f32[5,1,128,512]{3,0,2,1:T(8,128)} %copy-done.3, f32[5,1,1,512]{3,0,2,1:T(8,128)} %collective-permute-done.9, f32[5,1,1,512]{3,0,2,1:T(8,128)} %collective-permute-done.8, f32[5,1,128,1]{3,0,2,1:T(8,128)} %copy.103, f32[5,1,128,511]{3,0,2,1:T(8,128)} %get-tuple-element.102, ...), kind=kOutput, calls=%fused_computation.62 | convolution fusion | flops 23265280 | bytes 5523044 | tf_op jit(solution)/shard_map/vw,wzar->vzar/dot_general | solution.py:43
  233.3 8.5 %fusion.46 = f32[5,1,128,512]{3,0,2,1:T(8,128)} fusion(f32[5,1,128,512]{3,0,2,1:T(8,128)S(1)} %get-tuple-element.114, f32[5,1,1,512]{3,0,2,1:T(8,128)} %collective-permute-done.1, f32[5,1,1,512]{3,0,2,1:T(8,128)} %collective-permute-done, f32[5,1,128,512]{3,0,2,1:T(8,128)} %fusion.26, f32[5,1,128,511]{3,0,2,1:T(8,128)} %get-tuple-element.100, ...), kind=kOutput, calls=%fused_computation.90 | convolution fusion | flops 23592960 | bytes 9190500 | tf_op jit(solution)/shard_map/wv,wzar->vzar/dot_general | solution.py:125
  245.2 12.6 %scatter-add.85 = f32[5,1,128,512]{3,0,2,1:T(8,128)} dynamic-update-slice(f32[5,1,128,512]{3,0,2,1:T(8,128)} %fusion.46, f32[5,1,128,1]{3,0,2,1:T(8,128)S(1)} %add_select_fusion.3, s32[]{:T(128)} %constant.201.clone.1, s32[]{:T(128)} %constant.201.clone.1, s32[]{:T(128)} %constant.201.clone.1, s32[]{:T(128)} %bitcast.33) | dynamic-update-slice | bytes 5124 | tf_op jit(solution)/shard_map/scatter-add | solution.py:134
  262.4 2.8 scatter_custom_fusion.2
  265.2 4.1 scatter_fusion.1
  269.4 2.8 fusion.132
  272.2 76.1 %reduce-scatter.7.cloned.1.call-done = f32[5,128]{0,1:T(8,128)} async-done(((f32[5,4096]{0,1:T(8,128)}), f32[5,128]{0,1:T(8,128)}) %reduce-scatter.7.cloned.1.call-update) | async-done | bytes 2576 | tf_op jit(solution)/shard_map/reduce_scatter | solution.py:63
  349.4 8.5 %fusion.19 = f32[5,1,128,512]{3,0,2,1:T(8,128)} fusion(f32[5,1,128,512]{3,0,2,1:T(8,128)} %scatter-add.85, f32[5,1,128,512]{3,0,2,1:T(8,128)S(1)} %broadcast_multiply_fusion.2, f32[5,1,1,512]{3,0,2,1:T(8,128)S(1)} %collective-permute-done.13, f32[5,1,1,512]{3,0,2,1:T(8,128)S(1)} %collective-permute-done.12, f32[5,1,128,511]{3,0,2,1:T(8,128)} %get-tuple-element.96, ...), kind=kOutput, calls=%fused_computation.53 | convolution fusion | flops 23592960 | bytes 7879780 | tf_op jit(solution)/shard_map/wv,wzar->vzar/dot_general | solution.py:125
  361.3 12.6 %scatter-add.88 = f32[5,1,128,512]{3,0,2,1:T(8,128)} dynamic-update-slice(f32[5,1,128,512]{3,0,2,1:T(8,128)} %fusion.19, f32[5,1,128,1]{3,0,2,1:T(8,128)S(1)} %add_select_fusion.2, s32[]{:T(128)} %constant.201.clone.1, s32[]{:T(128)} %constant.201.clone.1, s32[]{:T(128)} %constant.201.clone.1, s32[]{:T(128)} %bitcast.33) | dynamic-update-slice | bytes 5124 | tf_op jit(solution)/shard_map/scatter-add | solution.py:134
  382.8 4.1 scatter_fusion.2
  387.0 2.8 fusion.130
  389.8 74.4 %reduce-scatter.9.cloned.1.call-done = f32[5,128]{0,1:T(8,128)} async-done(((f32[5,4096]{0,1:T(8,128)}), f32[5,128]{0,1:T(8,128)}) %reduce-scatter.9.cloned.1.call-update) | async-done | bytes 2576 | tf_op jit(solution)/shard_map/reduce_scatter | solution.py:63
  465.7 8.5 %fusion.13 = f32[5,1,128,512]{3,0,2,1:T(8,128)} fusion(f32[5,1,128,512]{3,0,2,1:T(8,128)} %scatter-add.88, f32[5,1,128,512]{3,0,2,1:T(8,128)S(1)} %broadcast_multiply_fusion.1, f32[5,1,1,512]{3,0,2,1:T(8,128)S(1)} %collective-permute-done.16, f32[5,1,1,512]{3,0,2,1:T(8,128)S(1)} %collective-permute-done.15, f32[5,1,128,511]{3,0,2,1:T(8,128)} %get-tuple-element.92, ...), kind=kOutput, calls=%fused_computation.45 | convolution fusion | flops 23592960 | bytes 7879780 | tf_op jit(solution)/shard_map/wv,wzar->vzar/dot_general | solution.py:125
  477.6 12.6 %scatter-add.91 = f32[5,1,128,512]{3,0,2,1:T(8,128)} dynamic-update-slice(f32[5,1,128,512]{3,0,2,1:T(8,128)} %fusion.13, f32[5,1,128,1]{3,0,2,1:T(8,128)S(1)} %add_select_fusion.1, s32[]{:T(128)} %constant.201.clone.1, s32[]{:T(128)} %constant.201.clone.1, s32[]{:T(128)} %constant.201.clone.1, s32[]{:T(128)} %bitcast.33) | dynamic-update-slice | bytes 5124 | tf_op jit(solution)/shard_map/scatter-add | solution.py:134
  493.1 2.8 fusion.128
  505.5 4.0 scatter_fusion.3
  511.6 22.8 %scatter_custom_fusion.8 = f32[3,32768]{0,1:T(8,128)} fusion(s32[3072]{0:T(1024)} %bitcast.234, f32[]{:T(128)} %constant.196.clone.1, f32[3,3072]{0,1:T(8,128)} %bitcast_multiply_fusion.4), kind=kCustom, calls=%fused_computation.29 | custom fusion | flops 9216 | bytes 1966592 | tf_op jit(solution)/shard_map/scatter-add | solution.py:147
  534.4 52.4 %reduce-scatter.11.cloned.1.call-done = f32[5,128]{0,1:T(8,128)} async-done(((f32[5,4096]{0,1:T(8,128)}), f32[5,128]{0,1:T(8,128)}) %reduce-scatter.11.cloned.1.call-update) | async-done | bytes 2576 | tf_op jit(solution)/shard_map/reduce_scatter | solution.py:63
  588.0 8.5 %fusion.7 = f32[5,1,128,512]{3,0,2,1:T(8,128)} fusion(f32[5,1,128,512]{3,0,2,1:T(8,128)} %scatter-add.91, f32[5,1,128,512]{3,0,2,1:T(8,128)S(1)} %broadcast_multiply_fusion, f32[5,1,1,512]{3,0,2,1:T(8,128)S(1)} %collective-permute-done.19, f32[5,1,1,512]{3,0,2,1:T(8,128)S(1)} %collective-permute-done.18, f32[5,1,128,511]{3,0,2,1:T(8,128)} %get-tuple-element.88, ...), kind=kOutput, calls=%fused_computation.37 | convolution fusion | flops 23592960 | bytes 7879780 | tf_op jit(solution)/shard_map/wv,wzar->vzar/dot_general | solution.py:125
  599.9 11.2 %scatter-add.94 = f32[5,1,128,512]{3,0,2,1:T(8,128)S(1)} dynamic-update-slice(f32[5,1,128,512]{3,0,2,1:T(8,128)S(1)} %copy-done.6, f32[5,1,128,1]{3,0,2,1:T(8,128)S(1)} %add_select_fusion, s32[]{:T(128)} %constant.201.clone.1, s32[]{:T(128)} %constant.201.clone.1, s32[]{:T(128)} %constant.201.clone.1, s32[]{:T(128)} %bitcast.33) | dynamic-update-slice | bytes 5124 | tf_op jit(solution)/shard_map/scatter-add | solution.py:134
  612.9 195.9 %all-reduce.13.cloned.1.call-done = f32[3,32768]{0,1:T(8,128)} async-done(((f32[3,32768]{0,1:T(8,128)}), f32[3,32768]{0,1:T(8,128)}) %all-reduce.13.cloned.1.call-update) | async-done | bytes 393232 | tf_op jit(solution)/shard_map/psum | solution.py:149
  (226 shorter events, 136.4 us)
Async XLA Ops:
  7.2 106.8 %copy-start = (f32[5,5]{1,0:T(8,128)S(1)}, f32[5,5]{1,0:T(8,128)}, u32[]{:S(2)}) copy-start(f32[5,5]{1,0:T(8,128)} %param.28) | copy-start | bytes 304
  7.2 225.3 %reduce-scatter.5.cloned.1.call-start = ((), (), s32[]{:S(2)}) async-start(), calls=%async_computation.4 | async-start | bytes 2162688 | tf_op jit(solution)/shard_map/reduce_scatter | solution.py:63
  9.9 63.8 %collective-permute-start.4 = (f32[5,128]{0,1:T(8,128)}, f32[5,128]{0,1:T(8,128)}, u32[]{:S(2)}, u32[]{:S(2)}) collective-permute-start(f32[5,128]{0,1:T(8,128)} %bitcast.3), channel_id=1, source_target_pairs={{0,32},{32,0},{64,96},{96,64},{1,33},{33,1},{65,97},{97,65},{2,34}... | collective-permute-start | bytes 7688 | tf_op jit(solution)/shard_map/ppermute | solution.py:12
  15.0 98.9 %collective-permute-start.2 = (f32[6,1,1,512]{3,0,2,1:T(8,128)}, f32[6,1,1,512]{3,0,2,1:T(8,128)}, u32[]{:S(2)}, u32[]{:S(2)}) collective-permute-start(f32[6,1,1,512]{3,0,2,1:T(8,128)} %get-tuple-element.85), channel_id=1, source_target_pairs={{1,0},{2,1},{3,2},{4,3},{5,4},{6,5},{7,6},{8,7},{9,8},{10,9},{11,1... | collective-permute-start | bytes 36872 | tf_op jit(solution)/shard_map/ppermute | solution.py:23
  15.9 98.0 %collective-permute-start.3 = (f32[6,1,1,512]{3,0,2,1:T(8,128)}, f32[6,1,1,512]{3,0,2,1:T(8,128)}, u32[]{:S(2)}, u32[]{:S(2)}) collective-permute-start(f32[6,1,1,512]{3,0,2,1:T(8,128)} %get-tuple-element.86), channel_id=1, source_target_pairs={{0,1},{1,2},{2,3},{3,4},{4,5},{5,6},{6,7},{7,8},{8,9},{9,10},{10,1... | collective-permute-start | bytes 36872 | tf_op jit(solution)/shard_map/ppermute | solution.py:22
  20.3 213.0 %collective-permute-start = (f32[5,1,1,512]{3,0,2,1:T(8,128)}, f32[5,1,1,512]{3,0,2,1:T(8,128)}, u32[]{:S(2)}, u32[]{:S(2)}) collective-permute-start(f32[5,1,1,512]{3,0,2,1:T(8,128)} %get-tuple-element.111), channel_id=1, source_target_pairs={{1,0},{2,1},{3,2},{4,3},{5,4},{6,5},{7,6},{8,7},{9,8},{10,9},{11,1... | collective-permute-start | bytes 30728 | tf_op jit(solution)/shard_map/ppermute | solution.py:23
  24.2 209.1 %collective-permute-start.1 = (f32[5,1,1,512]{3,0,2,1:T(8,128)}, f32[5,1,1,512]{3,0,2,1:T(8,128)}, u32[]{:S(2)}, u32[]{:S(2)}) collective-permute-start(f32[5,1,1,512]{3,0,2,1:T(8,128)} %get-tuple-element.112), channel_id=1, source_target_pairs={{0,1},{1,2},{2,3},{3,4},{4,5},{5,6},{6,7},{7,8},{8,9},{9,10},{10,1... | collective-permute-start | bytes 30728 | tf_op jit(solution)/shard_map/ppermute | solution.py:22
  40.8 307.5 %reduce-scatter.7.cloned.1.call-start = ((), (), s32[]{:S(2)}) async-start(), calls=%async_computation.5 | async-start | bytes 2162688 | tf_op jit(solution)/shard_map/reduce_scatter | solution.py:63
  59.4 11.7 %copy-start.25 = (s32[4]{0:T(128)S(1)}, s32[4]{0:T(128)}, u32[]{:S(2)}) copy-start(s32[4]{0:T(128)} %constant.207.clone.1) | copy-start | bytes 52
  59.4 13.7 %copy-start.24 = (f32[1,384]{1,0:T(1,128)S(1)}, f32[1,384]{1,0:T(1,128)}, u32[]{:S(2)}) copy-start(f32[1,384]{1,0:T(1,128)} %param.30) | copy-start | bytes 4612
  128.3 4.5 collective-permute-start.7
  130.6 38.0 %collective-permute-start.5 = (f32[5,1,1,512]{3,0,2,1:T(8,128)}, f32[5,1,1,512]{3,0,2,1:T(8,128)}, u32[]{:S(2)}, u32[]{:S(2)}) collective-permute-start(f32[5,1,1,512]{3,0,2,1:T(8,128)} %get-tuple-element.107), channel_id=1, source_target_pairs={{1,0},{2,1},{3,2},{4,3},{5,4},{6,5},{7,6},{8,7},{9,8},{10,9},{11,1... | collective-permute-start | bytes 30728 | tf_op jit(solution)/shard_map/ppermute | solution.py:23
  131.5 37.1 %collective-permute-start.6 = (f32[5,1,1,512]{3,0,2,1:T(8,128)}, f32[5,1,1,512]{3,0,2,1:T(8,128)}, u32[]{:S(2)}, u32[]{:S(2)}) collective-permute-start(f32[5,1,1,512]{3,0,2,1:T(8,128)} %get-tuple-element.108), channel_id=1, source_target_pairs={{0,1},{1,2},{2,3},{3,4},{4,5},{5,6},{6,7},{7,8},{8,9},{9,10},{10,1... | collective-permute-start | bytes 30728 | tf_op jit(solution)/shard_map/ppermute | solution.py:22
  182.9 3.7 collective-permute-start.10
  184.9 37.6 %collective-permute-start.8 = (f32[5,1,1,512]{3,0,2,1:T(8,128)}, f32[5,1,1,512]{3,0,2,1:T(8,128)}, u32[]{:S(2)}, u32[]{:S(2)}) collective-permute-start(f32[5,1,1,512]{3,0,2,1:T(8,128)} %get-tuple-element.103), channel_id=1, source_target_pairs={{1,0},{2,1},{3,2},{4,3},{5,4},{6,5},{7,6},{8,7},{9,8},{10,9},{11,1... | collective-permute-start | bytes 30728 | tf_op jit(solution)/shard_map/ppermute | solution.py:23
  185.3 37.2 %collective-permute-start.9 = (f32[5,1,1,512]{3,0,2,1:T(8,128)}, f32[5,1,1,512]{3,0,2,1:T(8,128)}, u32[]{:S(2)}, u32[]{:S(2)}) collective-permute-start(f32[5,1,1,512]{3,0,2,1:T(8,128)} %get-tuple-element.104), channel_id=1, source_target_pairs={{0,1},{1,2},{2,3},{3,4},{4,5},{5,6},{6,7},{7,8},{8,9},{9,10},{10,1... | collective-permute-start | bytes 30728 | tf_op jit(solution)/shard_map/ppermute | solution.py:22
  232.5 9.4 %collective-permute-start.11 = (f32[5,128]{0,1:T(8,128)}, f32[5,128]{0,1:T(8,128)S(1)}, u32[]{:S(2)}, u32[]{:S(2)}) collective-permute-start(f32[5,128]{0,1:T(8,128)} %reduce-scatter.5.cloned.1.call-done), channel_id=1, source_target_pairs={{0,32},{32,0},{64,96},{96,64},{1,33},{33,1},{65,97},{97,65},{2,34}... | collective-permute-start | bytes 7688 | tf_op jit(solution)/shard_map/ppermute | solution.py:12
  241.8 16.0 %copy-start.9 = (f32[1,128,512]{2,1,0:T(8,128)S(1)}, f32[1,128,512]{2,1,0:T(8,128)}, u32[]{:S(2)}) copy-start(f32[1,128,512]{2,1,0:T(8,128)} %param.25) | copy-start | bytes 786436
  260.1 89.3 %collective-permute-start.12 = (f32[5,1,1,512]{3,0,2,1:T(8,128)S(1)}, f32[5,1,1,512]{3,0,2,1:T(8,128)S(1)}, u32[]{:S(2)}, u32[]{:S(2)}) collective-permute-start(f32[5,1,1,512]{3,0,2,1:T(8,128)S(1)} %get-tuple-element.97), channel_id=1, source_target_pairs={{1,0},{2,1},{3,2},{4,3},{5,4},{6,5},{7,6},{8,7},{9,8},{10,9},{11,1... | collective-permute-start | bytes 30728 | tf_op jit(solution)/shard_map/ppermute | solution.py:23
  260.6 88.8 %collective-permute-start.13 = (f32[5,1,1,512]{3,0,2,1:T(8,128)S(1)}, f32[5,1,1,512]{3,0,2,1:T(8,128)S(1)}, u32[]{:S(2)}, u32[]{:S(2)}) collective-permute-start(f32[5,1,1,512]{3,0,2,1:T(8,128)S(1)} %get-tuple-element.98), channel_id=1, source_target_pairs={{0,1},{1,2},{2,3},{3,4},{4,5},{5,6},{6,7},{7,8},{8,9},{9,10},{10,1... | collective-permute-start | bytes 30728 | tf_op jit(solution)/shard_map/ppermute | solution.py:22
  269.3 194.8 %reduce-scatter.9.cloned.1.call-start = ((), (), s32[]{:S(2)}) async-start(), calls=%async_computation.6 | async-start | bytes 2162688 | tf_op jit(solution)/shard_map/reduce_scatter | solution.py:63
  348.2 9.7 %collective-permute-start.14 = (f32[5,128]{0,1:T(8,128)}, f32[5,128]{0,1:T(8,128)S(1)}, u32[]{:S(2)}, u32[]{:S(2)}) collective-permute-start(f32[5,128]{0,1:T(8,128)} %reduce-scatter.7.cloned.1.call-done), channel_id=1, source_target_pairs={{0,32},{32,0},{64,96},{96,64},{1,33},{33,1},{65,97},{97,65},{2,34}... | collective-permute-start | bytes 7688 | tf_op jit(solution)/shard_map/ppermute | solution.py:12
  376.2 89.5 %collective-permute-start.15 = (f32[5,1,1,512]{3,0,2,1:T(8,128)S(1)}, f32[5,1,1,512]{3,0,2,1:T(8,128)S(1)}, u32[]{:S(2)}, u32[]{:S(2)}) collective-permute-start(f32[5,1,1,512]{3,0,2,1:T(8,128)S(1)} %get-tuple-element.93), channel_id=1, source_target_pairs={{1,0},{2,1},{3,2},{4,3},{5,4},{6,5},{7,6},{8,7},{9,8},{10,9},{11,1... | collective-permute-start | bytes 30728 | tf_op jit(solution)/shard_map/ppermute | solution.py:23
  378.9 86.8 %collective-permute-start.16 = (f32[5,1,1,512]{3,0,2,1:T(8,128)S(1)}, f32[5,1,1,512]{3,0,2,1:T(8,128)S(1)}, u32[]{:S(2)}, u32[]{:S(2)}) collective-permute-start(f32[5,1,1,512]{3,0,2,1:T(8,128)S(1)} %get-tuple-element.94), channel_id=1, source_target_pairs={{0,1},{1,2},{2,3},{3,4},{4,5},{5,6},{6,7},{7,8},{8,9},{9,10},{10,1... | collective-permute-start | bytes 30728 | tf_op jit(solution)/shard_map/ppermute | solution.py:22
  386.9 199.8 %reduce-scatter.11.cloned.1.call-start = ((), (), s32[]{:S(2)}) async-start(), calls=%async_computation.7 | async-start | bytes 2162688 | tf_op jit(solution)/shard_map/reduce_scatter | solution.py:63
  464.1 10.1 %collective-permute-start.17 = (f32[5,128]{0,1:T(8,128)}, f32[5,128]{0,1:T(8,128)S(1)}, u32[]{:S(2)}, u32[]{:S(2)}) collective-permute-start(f32[5,128]{0,1:T(8,128)} %reduce-scatter.9.cloned.1.call-done), channel_id=1, source_target_pairs={{0,32},{32,0},{64,96},{96,64},{1,33},{33,1},{65,97},{97,65},{2,34}... | collective-permute-start | bytes 7688 | tf_op jit(solution)/shard_map/ppermute | solution.py:12
  498.3 7.2 copy-start.14
  498.9 89.1 %collective-permute-start.18 = (f32[5,1,1,512]{3,0,2,1:T(8,128)}, f32[5,1,1,512]{3,0,2,1:T(8,128)S(1)}, u32[]{:S(2)}, u32[]{:S(2)}) collective-permute-start(f32[5,1,1,512]{3,0,2,1:T(8,128)} %get-tuple-element.89), channel_id=1, source_target_pairs={{1,0},{2,1},{3,2},{4,3},{5,4},{6,5},{7,6},{8,7},{9,8},{10,9},{11,1... | collective-permute-start | bytes 30728 | tf_op jit(solution)/shard_map/ppermute | solution.py:23
  501.6 86.4 %collective-permute-start.19 = (f32[5,1,1,512]{3,0,2,1:T(8,128)S(1)}, f32[5,1,1,512]{3,0,2,1:T(8,128)S(1)}, u32[]{:S(2)}, u32[]{:S(2)}) collective-permute-start(f32[5,1,1,512]{3,0,2,1:T(8,128)S(1)} %get-tuple-element.90), channel_id=1, source_target_pairs={{0,1},{1,2},{2,3},{3,4},{4,5},{5,6},{6,7},{7,8},{8,9},{9,10},{10,1... | collective-permute-start | bytes 30728 | tf_op jit(solution)/shard_map/ppermute | solution.py:22
  509.6 299.3 %all-reduce.13.cloned.1.call-start = ((), (), s32[]{:S(2)}) async-start(), calls=%async_computation.8 | async-start | bytes 33554432 | tf_op jit(solution)/shard_map/psum | solution.py:149
  534.4 53.7 %copy-start.5 = (f32[5,1,128,512]{3,2,1,0:T(8,128)S(1)}, f32[5,1,128,512]{3,2,1,0:T(8,128)}, u32[]{:S(2)}) copy-start(f32[5,1,128,512]{3,2,1,0:T(8,128)} %param.24) | copy-start | bytes 3932164
  586.8 9.8 %collective-permute-start.20 = (f32[5,128]{0,1:T(8,128)}, f32[5,128]{0,1:T(8,128)S(1)}, u32[]{:S(2)}, u32[]{:S(2)}) collective-permute-start(f32[5,128]{0,1:T(8,128)} %reduce-scatter.11.cloned.1.call-done), channel_id=1, source_target_pairs={{0,32},{32,0},{64,96},{96,64},{1,33},{33,1},{65,97},{97,65},{2,34}... | collective-permute-start | bytes 7688 | tf_op jit(solution)/shard_map/ppermute | solution.py:12
  (20 other events, 93.8 us)
Sparse Core Ops, SparseCore 0:
  40.9 83.3 reduce-scatter.4
  269.5 78.7 reduce-scatter.6
  387.1 77.0 reduce-scatter.8
  509.7 77.0 reduce-scatter.10
  592.0 216.7 all-reduce.12
where the time goes:
time: 825 us; the launch traced here: 817 us
  waiting for transfers between devices  399 us (48%)
  local copies, waits for them, and re-layouts  137 us (17%)
  blocking collectives  90.4 us (11%)
  other arithmetic  87.3 us (11%)
  matrix products  60.5 us (7%)
  starting transfers between devices  28.4 us (3%)
  between operations  14.5 us (2%)
    reduce_scatter x4, waiting for transfers between devices, return_face(): lax.psum_scatter(collected, 'block', scatter_dimension=1, tiled=True)  203 us
    psum x1, waiting for transfers between devices, local(): summed = lax.psum(accumulated, ('zone', 'block'))  196 us
    all_gather x3, blocking collectives, gather_face(): partner_face = lax.all_gather(mirrored, 'block', axis=1, tiled=True)  90.4 us
    scatter-add x4, local copies, waits for them, and re-layouts, local(): adjoint = adjoint.at[:, 0, :, radial - 1].add(face_back)  49.1 us
    dot_general x4, matrix products, local(): jnp.einsum('wv,wzar->vzar', coupling, adjoint, precision=lax.Precision.HI...  34 us
    dot_general x3, matrix products, advance(): jnp.einsum('vw,wzar->vzar', coupling, jnp.tanh(middle), precision=lax.Pre...  26.3 us
    scatter-add x1, other arithmetic, local(): accumulated = jnp.zeros((3, point_total), jnp.float32).at[:, center_ids[0...  22.8 us
    scatter-add x4, other arithmetic, return_face(): collected.at[:, second_donor].add((1.0 - donor_part) * ghost_adjoint)  16.6 us
  transfers between devices with their start and end apart: 26, of which 4 were waited for; matrix products, arithmetic and copies ran while one was open for 27% of the time, Pallas kernels for 0%

commit v1 on v0

v1 whole, which is shorter than its diff:
```python
import functools

import jax
import jax.numpy as jnp
from jax import lax
from jax.experimental import pallas as pl
from jax.experimental.pallas import tpu as pltpu
from jax.sharding import PartitionSpec as P

MESH = pl.DeviceIdType.MESH
F32 = jnp.float32
V = 5
KU = 6
KL = 4
OFF_L = V * KU
OFF_K = OFF_L + V * KL
OFF_M = OFF_K + KU
OFF_W = OFF_M + 4
CHUNK = 64
ROWS = 160


def lane_of(shape):
    return lax.broadcasted_iota(jnp.int32, shape, len(shape) - 1)


def place():
    y = lax.axis_index("zone")
    b = lax.axis_index("block")
    return y, b, b // 8, (b // 2) % 4, b % 2


def block_of(x, z, c):
    return x * 8 + z * 2 + c


def remote(src, dst, send, recv, y, b):
    return pltpu.make_async_remote_copy(
        src_ref=src, dst_ref=dst, send_sem=send, recv_sem=recv, device_id=(y, b), device_id_type=MESH
    )


def exchange_kernel(
    u_hbm, k_hbm, l_hbm, m_hbm, w_hbm, gat, hu, hl, hk,
    chunk, ut, lt, kt, mt, wt, local_sem, halo_s, halo_r, first_s, first_r, ph_s, ph_r, core_s, core_r,
):
    y, b, x, z, c = place()
    q = y % 2
    yp = y + 1 - 2 * q
    b0 = b - c
    nxt, prv = (b + 1) % 32, (b + 31) % 32

    loads = [
        pltpu.make_async_copy(u_hbm.at[:, 0, :, pl.ds(384, 128)], ut, local_sem.at[0]),
        pltpu.make_async_copy(l_hbm.at[:, 0, :, pl.ds(384, 128)], lt, local_sem.at[1]),
        pltpu.make_async_copy(k_hbm.at[0, :, pl.ds(384, 128)], kt, local_sem.at[2]),
        pltpu.make_async_copy(m_hbm.at[:, 0, pl.ds(pl.multiple_of(b * 128, 128), 128)], mt, local_sem.at[3]),
        pltpu.make_async_copy(w_hbm.at[:, 0, pl.ds(pl.multiple_of(b * 128, 128), 128)], wt, local_sem.at[4]),
    ]
    for copy in loads:
        copy.start()

    barrier = pltpu.get_barrier_semaphore()
    peers = [(y, nxt), (y, prv), (yp, b0), (yp, b0 + 1), (y, b0 + 1 - c)]
    for d in (1, 2, 3):
        peers.append((y, block_of((x + d) % 4, z, c)))
        peers.append((y, block_of(x, (z + d) % 4, c)))
    for peer in peers:
        pl.semaphore_signal(barrier, inc=1, device_id=peer, device_id_type=MESH)
    pl.semaphore_wait(barrier, len(peers))

    halo = []
    for n, (src, dst) in enumerate(((u_hbm, hu), (l_hbm, hl), (k_hbm, hk))):
        def rows(r):
            return src.at[:, 0, pl.ds(r, 8), :] if len(src.shape) == 4 else src.at[0, pl.ds(r, 8), :]
        halo.append(remote(rows(120), dst.at[0], halo_s.at[n], halo_r.at[n], y, nxt))
        halo.append(remote(rows(0), dst.at[1], halo_s.at[3 + n], halo_r.at[3 + n], y, prv))
    for copy in halo:
        copy.start()

    for copy in loads:
        copy.wait()
    for v in range(V):
        chunk[KU * v : KU * (v + 1), :] = ut[v].T[128 - KU :, :]
        chunk[OFF_L + KL * v : OFF_L + KL * (v + 1), :] = lt[v].T[128 - KL :, :]
    chunk[OFF_K : OFF_K + KU, :] = kt[...].T[128 - KU :, :]
    chunk[OFF_M : OFF_M + 4, :] = mt[...].astype(F32)
    chunk[OFF_W : OFF_W + 4, :] = wt[...]

    def slot(zone, xx, j):
        return gat.at[zone, xx, j]

    here = slot(q, x, z * 2 + c)
    across = remote(chunk, here, first_s.at[0], first_r.at[c], yp, b0 + q)
    across.start()
    beside = remote(chunk, here, first_s.at[1], first_r.at[2], y, b0 + q)

    @pl.when(c == q)
    def _():
        gat[q, x, z * 2 + c] = chunk[...]
        remote(chunk, slot(q, x, z * 2 + 1 - c), first_s.at[1], first_r.at[2], y, b0 + q).wait_recv()

    @pl.when(c != q)
    def _():
        beside.start()
        for j in range(2):
            remote(chunk, slot(1 - q, x, z * 2 + j), first_s.at[0], first_r.at[j], yp, b0 + q).wait_recv()
        beside.wait_send()

    across.wait_send()

    def along(part_first, part_second, first_is_x):
        for stage in range(2):
            use_x = first_is_x == (stage == 0)
            copies = []
            for d in (1, 2, 3):
                to = block_of((x + d) % 4, z, c) if use_x else block_of(x, (z + d) % 4, c)
                src = (part_first if stage == 0 else part_second)(x, z)
                copies.append(remote(src, src, ph_s.at[3 * stage + d - 1], ph_r.at[3 * stage + d - 1], y, to))
            for copy in copies:
                copy.start()
            for copy in copies:
                copy.wait()

    @pl.when(c == 0)
    def _():
        along(lambda xx, zz: gat.at[0, xx, pl.ds(zz * 2, 2)], lambda xx, zz: gat.at[0, :, pl.ds(zz * 2, 2)], True)

    @pl.when(c == 1)
    def _():
        along(lambda xx, zz: gat.at[1, xx, pl.ds(zz * 2, 2)], lambda xx, zz: gat.at[1, xx], False)

    swap = remote(gat.at[c], gat.at[c], core_s, core_r, y, b0 + 1 - c)
    swap.start()
    swap.wait()
    for copy in halo:
        copy.wait()


def exchange(u, kappa, lam, dmap, dweight):
    any_ = pl.BlockSpec(memory_space=pl.ANY)
    vmem = pl.BlockSpec(memory_space=pltpu.VMEM)
    dma = pltpu.SemaphoreType.DMA
    return pl.pallas_call(
        exchange_kernel,
        out_shape=(
            jax.ShapeDtypeStruct((2, 4, 8, CHUNK, 128), F32),
            jax.ShapeDtypeStruct((2, V, 8, 512), F32),
            jax.ShapeDtypeStruct((2, V, 8, 512), F32),
            jax.ShapeDtypeStruct((2, 8, 512), F32),
        ),
        in_specs=[any_] * 5,
        out_specs=(vmem,) * 4,
        scratch_shapes=[
            pltpu.VMEM((CHUNK, 128), F32),
            pltpu.VMEM((V, 128, 128), F32),
            pltpu.VMEM((V, 128, 128), F32),
            pltpu.VMEM((128, 128), F32),
            pltpu.VMEM((4, 128), jnp.int32),
            pltpu.VMEM((4, 128), F32),
            dma((5,)), dma((6,)), dma((6,)), dma((2,)), dma((3,)), dma((6,)), dma((6,)), dma, dma,
        ],
        compiler_params=pltpu.CompilerParams(collective_id=0, has_side_effects=True),
        name="exchange",
    )(u, kappa, lam, dmap, dweight)


def fill_tiles(dst, src_vmem, halo, variables):
    pass


def main_forward(n, us, ds, kap, coup, tiles, ghost):
    lane = lane_of((8, 128))
    cf = [[coup[v, w] for w in range(V)] for v in range(V)]
    src, dst, dd = us[n], us[n + 1], ds[n]

    def body(i, carry):
        r = pl.multiple_of(8 + i * 8, 8)
        rows = pl.ds(r, 8)
        for t in tiles:
            k = kap[t, rows, :]
            cur = [src[v, t, rows, :] for v in range(V)]
            th = [jnp.tanh(a) for a in cur]
            for v in range(V):
                if t == 0:
                    left = jnp.where(lane == 127, 0.0, cur[v])
                else:
                    left = jnp.where(lane == 127, src[v, t - 1, rows, :], cur[v])
                if t < 3:
                    right = jnp.where(lane == 0, src[v, t + 1, rows, :], cur[v])
                elif ghost is None:
                    right = jnp.where(lane == 0, 0.0, cur[v])
                else:
                    g = pltpu.roll(ghost[rows, :], (128 - (n * V + v)) % 128, 1)
                    right = jnp.where(lane == 0, g, cur[v])
                lap = (
                    src[v, t, pl.ds(r - 1, 8), :] + src[v, t, pl.ds(r + 1, 8), :]
                    + pltpu.roll(left, 1, 1) + pltpu.roll(right, 127, 1) - 4.0 * cur[v]
                )
                react = cf[v][0] * th[0]
                for w in range(1, V):
                    react = react + cf[v][w] * th[w]
                dst[v, t, rows, :] = cur[v] + k * lap - react
                dd[v, t, rows, :] = 1.0 - th[v] * th[v]
        return carry

    lax.fori_loop(0, 18, body, 0)


def main_adjoint(n, us, ds, ls, ss, kap, coup, tiles, back, hsum, out):
    lane = lane_of((8, 128))
    cf = [[coup[w, v] for w in range(V)] for v in range(V)]
    m = 3 - n
    lam, sca = ls[m], ss[m]

    def body(i, carry):
        r = pl.multiple_of(8 + i * 8, 8)
        rows = pl.ds(r, 8)
        for t in tiles:
            cur = [lam[v, t, rows, :] for v in range(V)]
            for v in range(V):
                s = sca[v, t, rows, :]
                if t == 0:
                    left = jnp.where(lane == 127, 0.0, s)
                else:
                    left = jnp.where(lane == 127, sca[v, t - 1, rows, :], s)
                right = jnp.where(lane == 0, sca[v, t + 1, rows, :] if t < 3 else 0.0, s)
                lap = (
                    sca[v, t, pl.ds(r - 1, 8), :] + sca[v, t, pl.ds(r + 1, 8), :]
                    + pltpu.roll(left, 1, 1) + pltpu.roll(right, 127, 1) - 4.0 * s
                )
                if n == 3:
                    th = jnp.tanh(us[3][v, t, rows, :])
                    d = 1.0 - th * th
                else:
                    d = ds[n][v, t, rows, :]
                pulled = cf[v][0] * cur[0]
                for w in range(1, V):
                    pulled = pulled + cf[v][w] * cur[w]
                new = cur[v] + lap - d * pulled
                if t == 3 and back is not None:
                    f = pltpu.roll(back[rows, :], 127 - (15 + n * V + v), 1)
                    new = new + jnp.where(lane == 127, f, 0.0)
                if n > 0:
                    ls[m + 1][v, t, rows, :] = new
                    ss[m + 1][v, t, rows, :] = kap[t, rows, :] * new
                else:
                    out[v, t, pl.ds(pl.multiple_of(r - 16, 8), 8), :] = new
                if t == 0 and hsum is not None:
                    p = cur[v] * us[n][v, t, rows, :]
                    if n == 3:
                        hsum[v, rows, :] = p
                    else:
                        hsum[v, rows, :] = hsum[v, rows, :] + p
        return carry

    if n > 0:
        lax.fori_loop(0, 18, body, 0)
    else:
        lax.fori_loop(1, 17, body, 0)


def rows_beside(a):
    lane = lane_of(a.shape)
    up = pltpu.roll(jnp.where(lane == 127, pltpu.roll(a, 1, 0), a), 1, 1)
    down = pltpu.roll(jnp.where(lane == 0, pltpu.roll(a, 31, 0), a), 127, 1)
    return up + down


def put_ring(ring, a):
    ring[0:32, :] = a
    ring[32:64, :] = a
    ring[64:72, :] = a[0:8]


def shifted(ring, amount):
    lane = lane_of((32, 128))
    high, low = amount // 128, amount % 128
    first = ring[pl.ds(high, 32), :]
    second = ring[pl.ds(high + 1, 32), :]
    return pltpu.roll(jnp.where(lane < low, second, first), (128 - low) % 128, 1)


def strips(gat, q, coup, su, sd, sl, sk, tap, shift, ring, tring, face):
    row = lax.broadcasted_iota(jnp.int32, (32, 128), 0) * 128 + lane_of((32, 128))

    def get(zone, j):
        return gat[zone, pl.ds(j, 32, stride=CHUNK), :]

    def unpack(zone, carry):
        for v in range(V):
            for k in range(KU):
                su[0, zone, v, k] = get(zone, v * KU + KU - 1 - k)
            for k in range(KL):
                sl[0, zone, v, k] = get(zone, OFF_L + v * KL + KL - 1 - k)
        for k in range(KU):
            sk[zone, k] = get(zone, OFF_K + KU - 1 - k)
        for n in range(4):
            d = get(zone, OFF_M + n).astype(jnp.int32) - row
            base = d[0:1, 0:1]
            d = d - base
            d = jnp.where(d > 2048, d - 4096, d)
            d = jnp.where(d > 2048, d - 4096, d)
            d = jnp.where(d < -2048, d + 4096, d)
            d = jnp.where(d < -2048, d + 4096, d)
            least = jnp.min(d)
            e = d - least
            w = get(zone, OFF_W + n)
            shift[zone, n] = (base[0, 0] + least + 8192) % 4096
            for j in range(6):
                tap[zone, n, j] = jnp.where(e == j, w, 0.0) + jnp.where(e == j - 1, 1.0 - w, 0.0)
        return carry

    lax.fori_loop(0, 2, unpack, 0)

    for n in range(3):
        def faces(zone, carry):
            for v in range(V):
                put_ring(ring.at[zone, v], su[n, zone, v, 0])
            return carry

        lax.fori_loop(0, 2, faces, 0)

        def step(zone, carry):
            ghost = [jnp.zeros((32, 128), F32)] * V
            t = shift[zone, n]
            for j in range(6):
                cj = tap[zone, n, j]
                for v in range(V):
                    ghost[v] = ghost[v] + cj * shifted(ring.at[1 - zone, v], (t + j) % 4096)
            for v in range(V):
                face[zone, n * V + v] = ghost[v]
            for k in range(KU - 1 - n):
                cur = [su[n, zone, v, k] for v in range(V)]
                th = [jnp.tanh(a) for a in cur]
                kk = sk[zone, k]
                for v in range(V):
                    outward = ghost[v] if k == 0 else su[n, zone, v, k - 1]
                    lap = rows_beside(cur[v]) + outward + su[n, zone, v, k + 1] - 4.0 * cur[v]
                    react = coup[v, 0] * th[0]
                    for w in range(1, V):
                        react = react + coup[v, w] * th[w]
                    su[n + 1, zone, v, k] = cur[v] + kk * lap - react
                    if k < n:
                        sd[n, zone, v, k] = 1.0 - th[v] * th[v]
            return carry

        lax.fori_loop(0, 2, step, 0)

    for n in (3, 2, 1, 0):
        m = 3 - n

        def taps(zone, carry):
            for v in range(V):
                put_ring(ring.at[zone, v], sk[zone, 0] * sl[m, zone, v, 0])
            return carry

        lax.fori_loop(0, 2, taps, 0)

        def back(zone, carry):
            other = 1 - zone
            acc = [jnp.zeros((32, 128), F32)] * V
            t = shift[other, n]
            for j in range(6):
                put_ring(tring, tap[other, n, j])
                amount = (8192 - t - j) % 4096
                cj = shifted(tring, amount)
                for v in range(V):
                    acc[v] = acc[v] + cj * shifted(ring.at[other, v], amount)
            for v in range(V):
                face[zone, 15 + n * V + v] = acc[v]
            for k in range(n):
                cur = [sl[m, zone, v, k] for v in range(V)]
                kk = sk[zone, k]
                for v in range(V):
                    s = kk * cur[v]
                    lap = rows_beside(s) + sk[zone, k + 1] * sl[m, zone, v, k + 1] - 4.0 * s
                    if k == 0:
                        lap = lap + acc[v]
                    else:
                        lap = lap + sk[zone, k - 1] * sl[m, zone, v, k - 1]
                    if n == 3:
                        th = jnp.tanh(su[3, zone, v, k])
                        d = 1.0 - th * th
                    else:
                        d = sd[n, zone, v, k]
                    pulled = coup[0, v] * cur[0]
                    for w in range(1, V):
                        pulled = pulled + coup[w, v] * cur[w]
                    sl[m + 1, zone, v, k] = cur[v] + lap - d * pulled
            return carry

        if n > 0:
            lax.fori_loop(0, 2, back, 0)
        else:
            back(q, 0)


def face_columns(face, q, b, cols):
    pad = jnp.zeros((128 - 35, 128), F32)
    for part, dst, size, lo in (((b + 31) % 32, 8, 8, 120), (b, 16, 128, 0), ((b + 1) % 32, 144, 8, 0)):
        rows = face[q, pl.ds(part, 35, stride=32), :]
        cols[dst : dst + size, :] = jnp.concatenate([rows, pad], axis=0).T[lo : lo + size, :]


def scatter_points(hsum, area, proj, ids, dist, partial):
    lane = lane_of((128, 128))
    hs = [hsum[v, 16:144, :] for v in range(V)]
    acc = jnp.zeros((128, 128), F32)
    for c in range(3):
        col = proj[c, 0] * hs[0]
        for v in range(1, V):
            col = col + proj[c, v] * hs[v]
        acc = acc + jnp.where(lane == c, pltpu.roll(col, c, 1), 0.0)
    spread = (
        lax.broadcasted_iota(jnp.int32, (128, 384), 1) // 3 == lax.broadcasted_iota(jnp.int32, (128, 384), 0)
    ).astype(F32)
    sens = lax.dot_general(
        acc, spread, (((0,), (0,)), ((), ())), precision=lax.Precision.HIGHEST, preferred_element_type=F32
    )
    sens = [sens[c : c + 1, :] * area[...] for c in range(3)]
    sub_a = lax.broadcasted_iota(jnp.int32, (128, 128), 0)
    sub_b = lax.broadcasted_iota(jnp.int32, (256, 128), 0)
    total = jnp.zeros((384, 256), F32)
    for k in range(8):
        dk = dist[k : k + 1, :]
        om = 1.0 - dk
        om = om * om
        phi = om * om * (4.0 * dk + 1.0)
        idk = ids[k : k + 1, :]
        for wt in range(3):
            cut = slice(wt * 128, (wt + 1) * 128)
            idt = idk[:, cut]
            ch = idt // 256
            rowid = (ch % 2) * 64 + ((ch // 8) % 4) * 16 + ((ch // 2) % 4) * 4 + ch // 32
            mask = sub_a == rowid
            high, low = [], []
            for c in range(3):
                val = phi[:, cut] * sens[c][:, cut]
                hi = val.astype(jnp.bfloat16).astype(F32)
                high.append(jnp.where(mask, hi, 0.0).astype(jnp.bfloat16))
                low.append(jnp.where(mask, val - hi, 0.0).astype(jnp.bfloat16))
            left = jnp.concatenate([jnp.concatenate(high, axis=0), jnp.concatenate(low, axis=0)], axis=1)
            onehot = jnp.where(sub_b == idt % 256, 1.0, 0.0).astype(jnp.bfloat16)
            right = jnp.concatenate([onehot, onehot], axis=1)
            total = total + lax.dot_general(
                left, right, (((1,), (1,)), ((), ())), preferred_element_type=F32
            )
    for c in range(3):
        partial[c] = total[c * 128 : (c + 1) * 128, :]


def local_kernel(
    coup, proj, u_hbm, k_hbm, l_hbm, gat, hu, hl, hk, area, ids, dist, out_hbm, partial,
    u0, u1, u2, u3, d0, d1, d2, l4, l3, l2, l1, s4, s3, s2, s1, kap, hsum, outv,
    su, sd, sl, sk, tap, ring, tring, face, cols, shift, sem, osem,
):
    y, b, x, z, c = place()
    q = y % 2
    us, ds, ls, ss = (u0, u1, u2, u3), (d0, d1, d2), (l4, l3, l2, l1), (s4, s3, s2, s1)
    loads = []
    for t in range(4):
        cut = pl.ds(t * 128, 128)
        own = pl.ds(16, 128)
        loads.append(pltpu.make_async_copy(u_hbm.at[:, 0, :, cut], u0.at[:, t, own, :], sem.at[3 * t]))
        loads.append(pltpu.make_async_copy(l_hbm.at[:, 0, :, cut], l4.at[:, t, own, :], sem.at[3 * t + 1]))
        loads.append(pltpu.make_async_copy(k_hbm.at[0, :, cut], kap.at[t, own, :], sem.at[3 * t + 2]))
    for copy in loads:
        copy.start()
    for t in range(4):
        cut = slice(t * 128, (t + 1) * 128)
        for side, r in ((0, 8), (1, 144)):
            kap[t, r : r + 8, :] = hk[side, :, cut]
            for v in range(V):
                u0[v, t, r : r + 8, :] = hu[side, v, :, cut]
                l4[v, t, r : r + 8, :] = hl[side, v, :, cut]
    for copy in loads:
        copy.wait()

    def scale(i, carry):
        rows = pl.ds(pl.multiple_of(8 + i * 8, 8), 8)
        for t in range(4):
            for v in range(V):
                s4[v, t, rows, :] = kap[t, rows, :] * l4[v, t, rows, :]
        return carry

    lax.fori_loop(0, 18, scale, 0)
    every = (0, 1, 2, 3)
    for n in range(3):
        main_forward(n, us, ds, kap, coup, every, None)
    for n in (3, 2, 1, 0):
        main_adjoint(n, us, ds, ls, ss, kap, coup, every, None, hsum, outv)
    scatter_points(hsum, area, proj, ids, dist, partial)
    strips(gat, q, coup, su, sd, sl, sk, tap, shift, ring, tring, face)
    face_columns(face.reshape(2, 35 * 32, 128), q, b, cols)
    for n in range(3):
        main_forward(n, us, ds, kap, coup, (3,), cols)
    for n in (3, 2, 1, 0):
        main_adjoint(n, us, ds, ls, ss, kap, coup, (3,), cols, None, outv)
    stores = []
    for t in range(4):
        stores.append(
            pltpu.make_async_copy(outv.at[:, t], out_hbm.at[:, 0, :, pl.ds(t * 128, 128)], osem.at[t])
        )
    for copy in stores:
        copy.start()
    for copy in stores:
        copy.wait()


def local_part(coup, proj, u, kappa, lam, gat, hu, hl, hk, area, ids, dist):
    any_ = pl.BlockSpec(memory_space=pl.ANY)
    vmem = pl.BlockSpec(memory_space=pltpu.VMEM)
    smem = pl.BlockSpec(memory_space=pltpu.SMEM)
    dma = pltpu.SemaphoreType.DMA
    cells = pltpu.VMEM((V, 4, ROWS, 128), F32)
    return pl.pallas_call(
        local_kernel,
        out_shape=(
            jax.ShapeDtypeStruct((V, 1, 128, 512), F32),
            jax.ShapeDtypeStruct((3, 128, 256), F32),
        ),
        in_specs=[smem, smem, any_, any_, any_, vmem, vmem, vmem, vmem, vmem, vmem, vmem],
        out_specs=(any_, vmem),
        scratch_shapes=[cells] * 15
        + [
            pltpu.VMEM((4, ROWS, 128), F32),
            pltpu.VMEM((V, ROWS, 128), F32),
            pltpu.VMEM((V, 4, 128, 128), F32),
            pltpu.VMEM((4, 2, V, KU, 32, 128), F32),
            pltpu.VMEM((3, 2, V, 2, 32, 128), F32),
            pltpu.VMEM((4, 2, V, KL, 32, 128), F32),
            pltpu.VMEM((2, KU, 32, 128), F32),
            pltpu.VMEM((2, 4, 6, 32, 128), F32),
            pltpu.VMEM((2, V, 72, 128), F32),
            pltpu.VMEM((72, 128), F32),
            pltpu.VMEM((2, 35, 32, 128), F32),
            pltpu.VMEM((ROWS, 128), F32),
            pltpu.SMEM((2, 4), jnp.int32),
            dma((12,)), dma((4,)),
        ],
        compiler_params=pltpu.CompilerParams(vmem_limit_bytes=62 * 1024 * 1024),
        name="cells",
    )(coup, proj, u, kappa, lam, gat.reshape(2, 32 * CHUNK, 128), hu, hl, hk, area, ids, dist)


def reduce_kernel(part, out, r1, q1, r2, q2, r3, q3, r4, ss, rs):
    y, b, x, z, c = place()
    barrier = pltpu.get_barrier_semaphore()
    peers = [(y, block_of(x, z, 1 - c))]
    for d in (1, 2, 3):
        peers.append((y, block_of((x + d) % 4, z, c)))
        peers.append((y, block_of(x, (z + d) % 4, c)))
        peers.append(((y + d) % 4, b))
    for peer in peers:
        pl.semaphore_signal(barrier, inc=1, device_id=peer, device_id_type=MESH)
    pl.semaphore_wait(barrier, len(peers))

    copy = remote(
        part.at[:, pl.ds(pl.multiple_of((1 - c) * 64, 64), 64), :], r1, ss.at[0], rs.at[0], y, block_of(x, z, 1 - c)
    )
    copy.start()
    copy.wait()
    own = pl.multiple_of(c * 64, 64)
    for j in range(4):
        q1[j] = part[:, pl.ds(own + j * 16, 16), :] + r1[:, j * 16 : (j + 1) * 16, :]

    copies = []
    for d in (1, 2, 3):
        to = (x + d) % 4
        copies.append(remote(q1.at[to], r2.at[d - 1], ss.at[d], rs.at[d], y, block_of(to, z, c)))
    for copy in copies:
        copy.start()
    for copy in copies:
        copy.wait()
    total = q1[x] + r2[0] + r2[1] + r2[2]
    for j in range(4):
        q2[j] = total[:, j * 4 : (j + 1) * 4, :]

    copies = []
    for d in (1, 2, 3):
        to = (z + d) % 4
        copies.append(remote(q2.at[to], r3.at[d - 1], ss.at[3 + d], rs.at[3 + d], y, block_of(x, to, c)))
    for copy in copies:
        copy.start()
    for copy in copies:
        copy.wait()
    total = q2[z] + r3[0] + r3[1] + r3[2]
    for j in range(4):
        q3[j] = total[:, j, :]

    copies = []
    for d in (1, 2, 3):
        to = (y + d) % 4
        copies.append(remote(q3.at[to], r4.at[d - 1], ss.at[6 + d], rs.at[6 + d], to, b))
    for copy in copies:
        copy.start()
    for copy in copies:
        copy.wait()
    out[...] = q3[y] + r4[0] + r4[1] + r4[2]


def reduce_points(partial):
    vmem = pl.BlockSpec(memory_space=pltpu.VMEM)
    dma = pltpu.SemaphoreType.DMA
    return pl.pallas_call(
        reduce_kernel,
        out_shape=jax.ShapeDtypeStruct((3, 256), F32),
        in_specs=[vmem],
        out_specs=vmem,
        scratch_shapes=[
            pltpu.VMEM((3, 64, 256), F32),
            pltpu.VMEM((4, 3, 16, 256), F32),
            pltpu.VMEM((3, 3, 16, 256), F32),
            pltpu.VMEM((4, 3, 4, 256), F32),
            pltpu.VMEM((3, 3, 4, 256), F32),
            pltpu.VMEM((4, 3, 256), F32),
            pltpu.VMEM((3, 3, 256), F32),
            dma((10,)), dma((10,)),
        ],
        compiler_params=pltpu.CompilerParams(collective_id=1, has_side_effects=True),
        name="reduce",
    )(partial)


def local(
    start_state, diffusivity, donor_map, donor_weight, coupling, final_cotangent,
    wall_area, wall_projection, center_ids, center_dist,
):
    gat, hu, hl, hk = exchange(start_state, diffusivity, final_cotangent, donor_map, donor_weight)
    adjoint, partial = local_part(
        coupling, wall_projection, start_state, diffusivity, final_cotangent, gat, hu, hl, hk,
        wall_area, center_ids[0], center_dist[0],
    )
    return adjoint, reduce_points(partial)


def solution(mesh):
    return jax.shard_map(
        local,
        mesh=mesh,
        in_specs=(
            P(None, "zone", "block", None),
            P("zone", "block", None),
            P(None, "zone", None),
            P(None, "zone", None),
            P(),
            P(None, "zone", "block", None),
            P("zone", "block"),
            P(),
            P("zone", None, "block"),
            P("zone", None, "block"),
        ),
        out_specs=(P(None, "zone", "block", None), P(None, ("zone", "block"))),
        check_vma=False,
    )
```

time: 825 us -> 91.6 us (0.11)
  waiting for transfers between devices: 399 us -> 0 us
  local copies, waits for them, and re-layouts: 137 us -> 1.27 us
  blocking collectives: 90.4 us -> 0 us
  Pallas kernels: 0 us -> 88.3 us
  other arithmetic: 87.3 us -> 0 us
  matrix products: 60.5 us -> 0 us
  starting transfers between devices: 28.4 us -> 0 us
  between operations: 14.5 us -> 0.65 us
    reduce_scatter x4 -> x0, waiting for transfers between devices: 203 us -> none  [return_face(): lax.psum_scatter(collected, 'block', scatter_dimension=1, tiled=True)]
    psum x1 -> x0, waiting for transfers between devices: 196 us -> none  [local(): summed = lax.psum(accumulated, ('zone', 'block'))]
    all_gather x3 -> x0, blocking collectives: 90.4 us -> none  [gather_face(): partner_face = lax.all_gather(mirrored, 'block', axis=1, tiled=True)]
    pallas_call x0 -> x3, Pallas kernels: none -> 88.3 us  [the longest x1 45.1 us: local_part(): pl.pallas_call(local_kernel, out_shape=(jax.ShapeDtypeStruct((V, 1, 128,...]
    dot_general x8 -> x0, matrix products: 60.5 us -> none  [the longest x4 34 us: local(): jnp.einsum('wv,wzar->vzar', coupling, adjoint, precision=lax.Precision.HI...]
    scatter-add x9 -> x0, other arithmetic: 50.1 us -> none  [the longest x1 22.8 us: local(): accumulated = jnp.zeros((3, point_total), jnp.float32).at[:, center_ids[0...]
    scatter-add x4 -> x0, local copies, waits for them, and re-layouts: 49.1 us -> none  [local(): adjoint = adjoint.at[:, 0, :, radial - 1].add(face_back)]
    slice x26 -> x0, local copies, waits for them, and re-layouts: 34.1 us -> none  [the longest x4 11.2 us: local(): scaled[..., 1:]]
  transfers between devices with their start and end apart: 26 -> 0, of which waited for: 4 -> 0; matrix products, arithmetic and copies ran while one was open for 27% -> 0% of each run, Pallas kernels for 0% -> 0%
where the time goes in v1:
time: 91.6 us; the launch traced here: 90.3 us
  Pallas kernels  88.3 us (96%)
  local copies, waits for them, and re-layouts  1.27 us (1%)
    pallas_call x1, Pallas kernels, local_part(): pl.pallas_call(local_kernel, out_shape=(jax.ShapeDtypeStruct((V, 1, 128,...  45.1 us
    pallas_call x1, Pallas kernels, exchange(): pl.pallas_call(exchange_kernel, out_shape=(jax.ShapeDtypeStruct((2, 4, 8,...  26.2 us
    pallas_call x1, Pallas kernels, reduce_points(): pl.pallas_call(reduce_kernel, out_shape=jax.ShapeDtypeStruct((3, 256), F3...  17 us

profile of v1, /device:TPU:1, one launch (start us, length us, event | category | flops | bytes accessed | tf_op | source)
XLA Modules:
  0.0 90.3 jit_solution(959354170294532321)
XLA Ops:
  0.6 26.2 %exchange.1 = (f32[2,4,8,64,128]{4,3,2,1,0:T(8,128)}, f32[2,5,8,512]{3,2,1,0:T(8,128)}, f32[2,5,8,512]{3,2,1,0:T(8,128)}, f32[2,8,512]{2,1,0:T(8,128)}) custom-call(f32[5,1,128,512]{3,2,1,0:T(8,128)} %u_hbm.3, f32[1,128,512]{2,1,0:T(8,128)} %k_hbm.3, f32[5,1,128,512]{3,2,1,0:T(8,128)} %l_hbm.3, s32[4,1,4096]{2,1,0:T(1,128)} %m_hbm.1, f32[4,1,4096]{2,1,0:T(1,128)} %w_hbm.1), custom_call_target="tpu_custom_call" | custom-call | tf_op jit(solution)/shard_map/exchange/pallas_call | solution.py:144
  26.9 45.1 %cells.1 = (f32[5,1,128,512]{3,2,1,0:T(8,128)}, f32[3,128,256]{2,1,0:T(8,128)}) custom-call(f32[5,5]{1,0:T(8,128)} %coup.1, f32[3,5]{1,0:T(4,128)} %proj.1, f32[5,1,128,512]{3,2,1,0:T(8,128)} %u_hbm.3, f32[1,128,512]{2,1,0:T(8,128)} %k_hbm.3, f32[5,1,128,512]{3,2,1,0:T(8,128)} %l_hbm.3, f32[2,2048,128]{2,1,0:T(8,128)} %bitcast.3, ...), custom_call_target="tpu_custom_call" | custom-call | tf_op jit(solution)/shard_map/cells/pallas_call | solution.py:517
  72.0 17.0 %reduce.1 = f32[3,256]{1,0:T(4,128)} custom-call(f32[3,128,256]{2,1,0:T(8,128)} %get-tuple-element.13.part), custom_call_target="tpu_custom_call" | custom-call | tf_op jit(solution)/shard_map/reduce/pallas_call | solution.py:606
  89.0 1.3 %copy.13 = f32[3,256]{1,0:T(4,128)} copy(f32[3,256]{1,0:T(4,128)} %reduce.1) | data formatting | bytes 6144

commit v2 on v1

v2 whole, which is shorter than its diff:
```python
import functools

import jax
import jax.numpy as jnp
from jax import lax
from jax.experimental import pallas as pl
from jax.experimental.pallas import tpu as pltpu
from jax.sharding import PartitionSpec as P

MESH = pl.DeviceIdType.MESH
F32 = jnp.float32
V = 5
KU = 6
KL = 4
OFF_L = V * KU
OFF_K = OFF_L + V * KL
OFF_M = OFF_K + KU
OFF_W = OFF_M + 4
CHUNK = 64
ROWS = 160


def lane_of(shape):
    return lax.broadcasted_iota(jnp.int32, shape, len(shape) - 1)


def place():
    y = lax.axis_index("zone")
    b = lax.axis_index("block")
    return y, b, b // 8, (b // 2) % 4, b % 2


def block_of(x, z, c):
    return x * 8 + z * 2 + c


def remote(src, dst, send, recv, y, b):
    return pltpu.make_async_remote_copy(
        src_ref=src, dst_ref=dst, send_sem=send, recv_sem=recv, device_id=(y, b), device_id_type=MESH
    )


def over_rows(body, first, count, unroll):
    def several(i, carry):
        for j in range(unroll):
            body(first + i * unroll + j)
        return carry

    lax.fori_loop(0, count // unroll, several, 0)


def main_forward(n, us, ds, kap, coup, tiles, ghost):
    lane = lane_of((8, 128))
    cf = [[coup[v, w] for w in range(V)] for v in range(V)]
    src, dst, dd = us[n], us[n + 1], ds[n]

    def body(i):
        r = pl.multiple_of(8 + i * 8, 8)
        rows = pl.ds(r, 8)
        for t in tiles:
            k = kap[t, rows, :]
            cur = [src[v, t, rows, :] for v in range(V)]
            th = [jnp.tanh(a) for a in cur]
            for v in range(V):
                if t == 0:
                    left = jnp.where(lane == 127, 0.0, cur[v])
                else:
                    left = jnp.where(lane == 127, src[v, t - 1, rows, :], cur[v])
                if t < 3:
                    right = jnp.where(lane == 0, src[v, t + 1, rows, :], cur[v])
                elif ghost is None:
                    right = jnp.where(lane == 0, 0.0, cur[v])
                else:
                    g = pltpu.roll(ghost[rows, :], (128 - (n * V + v)) % 128, 1)
                    right = jnp.where(lane == 0, g, cur[v])
                lap = (
                    src[v, t, pl.ds(r - 1, 8), :] + src[v, t, pl.ds(r + 1, 8), :]
                    + pltpu.roll(left, 1, 1) + pltpu.roll(right, 127, 1) - 4.0 * cur[v]
                )
                react = cf[v][0] * th[0]
                for w in range(1, V):
                    react = react + cf[v][w] * th[w]
                dst[v, t, rows, :] = cur[v] + k * lap - react
                dd[v, t, rows, :] = 1.0 - th[v] * th[v]

    over_rows(body, 0, 18, 6 if len(tiles) == 1 else 2)


def main_adjoint(n, us, ds, ls, ss, kap, coup, tiles, back, hsum, out):
    lane = lane_of((8, 128))
    cf = [[coup[w, v] for w in range(V)] for v in range(V)]
    m = 3 - n
    lam, sca = ls[m], ss[m]

    def body(i):
        r = pl.multiple_of(8 + i * 8, 8)
        rows = pl.ds(r, 8)
        for t in tiles:
            cur = [lam[v, t, rows, :] for v in range(V)]
            for v in range(V):
                s = sca[v, t, rows, :]
                if t == 0:
                    left = jnp.where(lane == 127, 0.0, s)
                else:
                    left = jnp.where(lane == 127, sca[v, t - 1, rows, :], s)
                right = jnp.where(lane == 0, sca[v, t + 1, rows, :] if t < 3 else 0.0, s)
                lap = (
                    sca[v, t, pl.ds(r - 1, 8), :] + sca[v, t, pl.ds(r + 1, 8), :]
                    + pltpu.roll(left, 1, 1) + pltpu.roll(right, 127, 1) - 4.0 * s
                )
                if n == 3:
                    th = jnp.tanh(us[3][v, t, rows, :])
                    d = 1.0 - th * th
                else:
                    d = ds[n][v, t, rows, :]
                pulled = cf[v][0] * cur[0]
                for w in range(1, V):
                    pulled = pulled + cf[v][w] * cur[w]
                new = cur[v] + lap - d * pulled
                if t == 3 and back is not None:
                    f = pltpu.roll(back[rows, :], 127 - (15 + n * V + v), 1)
                    new = new + jnp.where(lane == 127, f, 0.0)
                if n > 0:
                    ls[m + 1][v, t, rows, :] = new
                    ss[m + 1][v, t, rows, :] = kap[t, rows, :] * new
                else:
                    out[v, t, pl.ds(pl.multiple_of(r - 16, 8), 8), :] = new
                if t == 0 and hsum is not None:
                    p = cur[v] * us[n][v, t, rows, :]
                    if n == 3:
                        hsum[v, rows, :] = p
                    else:
                        hsum[v, rows, :] = hsum[v, rows, :] + p

    if n > 0:
        over_rows(body, 0, 18, 6 if len(tiles) == 1 else 2)
    else:
        over_rows(body, 1, 16, 4 if len(tiles) == 1 else 2)


def rows_beside(a):
    lane = lane_of(a.shape)
    up = pltpu.roll(jnp.where(lane == 127, pltpu.roll(a, 1, 0), a), 1, 1)
    down = pltpu.roll(jnp.where(lane == 0, pltpu.roll(a, 31, 0), a), 127, 1)
    return up + down


def put_ring(ring, a):
    ring[0:32, :] = a
    ring[32:64, :] = a
    ring[64:72, :] = a[0:8]


def shifted(ring, amount):
    lane = lane_of((32, 128))
    high, low = amount // 128, amount % 128
    first = ring[pl.ds(high, 32), :]
    second = ring[pl.ds(high + 1, 32), :]
    return pltpu.roll(jnp.where(lane < low, second, first), (128 - low) % 128, 1)


def strips(gat, q, coup, su, sd, sl, sk, tap, shift, ring, tring, face, between):
    row = lax.broadcasted_iota(jnp.int32, (32, 128), 0) * 128 + lane_of((32, 128))

    def get(zone, j):
        return gat[zone, pl.ds(j, 32, stride=CHUNK), :]

    def unpack(zone, carry):
        for v in range(V):
            for k in range(KU):
                su[0, zone, v, k] = get(zone, v * KU + KU - 1 - k)
            for k in range(KL):
                sl[0, zone, v, k] = get(zone, OFF_L + v * KL + KL - 1 - k)
        for k in range(KU):
            sk[zone, k] = get(zone, OFF_K + KU - 1 - k)
        for n in range(4):
            d = get(zone, OFF_M + n).astype(jnp.int32) - row
            base = d[0:1, 0:1]
            d = d - base
            d = jnp.where(d > 2048, d - 4096, d)
            d = jnp.where(d > 2048, d - 4096, d)
            d = jnp.where(d < -2048, d + 4096, d)
            d = jnp.where(d < -2048, d + 4096, d)
            least = jnp.min(d)
            e = d - least
            w = get(zone, OFF_W + n)
            shift[zone, n] = (base[0, 0] + least + 8192) % 4096
            for j in range(6):
                tap[zone, n, j] = jnp.where(e == j, w, 0.0) + jnp.where(e == j - 1, 1.0 - w, 0.0)
        return carry

    lax.fori_loop(0, 2, unpack, 0)

    for n in range(3):
        def faces(zone, carry):
            for v in range(V):
                put_ring(ring.at[zone, v], su[n, zone, v, 0])
            return carry

        lax.fori_loop(0, 2, faces, 0)

        def step(zone, carry):
            ghost = [jnp.zeros((32, 128), F32)] * V
            t = shift[zone, n]
            for j in range(6):
                cj = tap[zone, n, j]
                for v in range(V):
                    ghost[v] = ghost[v] + cj * shifted(ring.at[1 - zone, v], (t + j) % 4096)
            for v in range(V):
                face[zone, n * V + v] = ghost[v]
            for k in range(KU - 1 - n):
                cur = [su[n, zone, v, k] for v in range(V)]
                th = [jnp.tanh(a) for a in cur]
                kk = sk[zone, k]
                for v in range(V):
                    outward = ghost[v] if k == 0 else su[n, zone, v, k - 1]
                    lap = rows_beside(cur[v]) + outward + su[n, zone, v, k + 1] - 4.0 * cur[v]
                    react = coup[v, 0] * th[0]
                    for w in range(1, V):
                        react = react + coup[v, w] * th[w]
                    su[n + 1, zone, v, k] = cur[v] + kk * lap - react
                    if k < n:
                        sd[n, zone, v, k] = 1.0 - th[v] * th[v]
            return carry

        lax.fori_loop(0, 2, step, 0)
        between(n)

    for n in (3, 2, 1, 0):
        m = 3 - n

        def taps(zone, carry):
            for v in range(V):
                put_ring(ring.at[zone, v], sk[zone, 0] * sl[m, zone, v, 0])
            return carry

        lax.fori_loop(0, 2, taps, 0)

        def back(zone, carry):
            other = 1 - zone
            acc = [jnp.zeros((32, 128), F32)] * V
            t = shift[other, n]
            for j in range(6):
                put_ring(tring, tap[other, n, j])
                amount = (8192 - t - j) % 4096
                cj = shifted(tring, amount)
                for v in range(V):
                    acc[v] = acc[v] + cj * shifted(ring.at[other, v], amount)
            for v in range(V):
                face[zone, 15 + n * V + v] = acc[v]
            for k in range(n):
                cur = [sl[m, zone, v, k] for v in range(V)]
                kk = sk[zone, k]
                for v in range(V):
                    s = kk * cur[v]
                    lap = rows_beside(s) + sk[zone, k + 1] * sl[m, zone, v, k + 1] - 4.0 * s
                    if k == 0:
                        lap = lap + acc[v]
                    else:
                        lap = lap + sk[zone, k - 1] * sl[m, zone, v, k - 1]
                    if n == 3:
                        th = jnp.tanh(su[3, zone, v, k])
                        d = 1.0 - th * th
                    else:
                        d = sd[n, zone, v, k]
                    pulled = coup[0, v] * cur[0]
                    for w in range(1, V):
                        pulled = pulled + coup[w, v] * cur[w]
                    sl[m + 1, zone, v, k] = cur[v] + lap - d * pulled
            return carry

        if n > 0:
            lax.fori_loop(0, 2, back, 0)
        else:
            back(q, 0)
        between(6 - n)


def face_columns(face, q, b, cols):
    pad = jnp.zeros((128 - 35, 128), F32)
    for part, dst, size, lo in (((b + 31) % 32, 8, 8, 120), (b, 16, 128, 0), ((b + 1) % 32, 144, 8, 0)):
        rows = face[q, pl.ds(part, 35, stride=32), :]
        cols[dst : dst + size, :] = jnp.concatenate([rows, pad], axis=0).T[lo : lo + size, :]


def scatter_points(hsum, area, proj, ids, dist, partial):
    lane = lane_of((128, 128))
    hs = [hsum[v, 16:144, :] for v in range(V)]
    acc = jnp.zeros((128, 128), F32)
    for c in range(3):
        col = proj[c, 0] * hs[0]
        for v in range(1, V):
            col = col + proj[c, v] * hs[v]
        acc = acc + jnp.where(lane == c, pltpu.roll(col, c, 1), 0.0)
    spread = (
        lax.broadcasted_iota(jnp.int32, (128, 384), 1) // 3 == lax.broadcasted_iota(jnp.int32, (128, 384), 0)
    ).astype(F32)
    sens = lax.dot_general(
        acc, spread, (((0,), (0,)), ((), ())), precision=lax.Precision.HIGHEST, preferred_element_type=F32
    )
    sens = [sens[c : c + 1, :] * area[...] for c in range(3)]
    sub_a = lax.broadcasted_iota(jnp.int32, (128, 128), 0)
    sub_b = lax.broadcasted_iota(jnp.int32, (256, 128), 0)
    total = jnp.zeros((384, 256), F32)
    for k in range(8):
        dk = dist[k : k + 1, :]
        om = 1.0 - dk
        om = om * om
        phi = om * om * (4.0 * dk + 1.0)
        idk = ids[k : k + 1, :]
        for wt in range(3):
            cut = slice(wt * 128, (wt + 1) * 128)
            idt = idk[:, cut]
            ch = idt // 256
            rowid = (ch % 2) * 64 + ((ch // 8) % 4) * 16 + ((ch // 2) % 4) * 4 + ch // 32
            mask = sub_a == rowid
            high, low = [], []
            for c in range(3):
                val = phi[:, cut] * sens[c][:, cut]
                hi = val.astype(jnp.bfloat16).astype(F32)
                high.append(jnp.where(mask, hi, 0.0).astype(jnp.bfloat16))
                low.append(jnp.where(mask, val - hi, 0.0).astype(jnp.bfloat16))
            left = jnp.concatenate([jnp.concatenate(high, axis=0), jnp.concatenate(low, axis=0)], axis=1)
            onehot = jnp.where(sub_b == idt % 256, 1.0, 0.0).astype(jnp.bfloat16)
            right = jnp.concatenate([onehot, onehot], axis=1)
            total = total + lax.dot_general(
                left, right, (((1,), (1,)), ((), ())), preferred_element_type=F32
            )
    for c in range(3):
        partial[c] = total[c * 128 : (c + 1) * 128, :]


def window_kernel(
    coup, proj, u_hbm, k_hbm, l_hbm, m_hbm, w_hbm, area, ids, dist, out_hbm, points,
    u0, u1, u2, u3, d0, d1, d2, l4, l3, l2, l1, s4, s3, s2, s1, kap, hsum, outv,
    su, sd, sl, sk, tap, ring, tring, face, cols, shift,
    gat, hu, hl, hk, chunk, mt, wt, partial, r1, q1, r2, q2, r3, q3, r4,
    sem, osem, halo_s, halo_r, first_s, first_r, ph_s, ph_r, core_s, core_r, rs_s, rs_r,
):
    y, b, x, z, c = place()
    q = y % 2
    yp = y + 1 - 2 * q
    b0 = b - c
    twin = b0 + 1 - c
    nxt, prv = (b + 1) % 32, (b + 31) % 32
    us, ds, ls, ss = (u0, u1, u2, u3), (d0, d1, d2), (l4, l3, l2, l1), (s4, s3, s2, s1)

    def loads_of(t):
        cut = pl.ds(t * 128, 128)
        own = pl.ds(16, 128)
        return [
            pltpu.make_async_copy(u_hbm.at[:, 0, :, cut], u0.at[:, t, own, :], sem.at[3 * t]),
            pltpu.make_async_copy(l_hbm.at[:, 0, :, cut], l4.at[:, t, own, :], sem.at[3 * t + 1]),
            pltpu.make_async_copy(k_hbm.at[0, :, cut], kap.at[t, own, :], sem.at[3 * t + 2]),
        ]

    mine = pl.ds(pl.multiple_of(b * 128, 128), 128)
    maps = [
        pltpu.make_async_copy(m_hbm.at[:, 0, mine], mt, sem.at[12]),
        pltpu.make_async_copy(w_hbm.at[:, 0, mine], wt, sem.at[13]),
    ]
    loads = [loads_of(t) for t in range(4)]
    for copy in loads[3] + maps + loads[0] + loads[1] + loads[2]:
        copy.start()

    barrier = pltpu.get_barrier_semaphore()
    peers = [(y, nxt), (y, prv), (yp, b0), (yp, b0 + 1), (y, twin)]
    for d in (1, 2, 3):
        peers.append((y, block_of((x + d) % 4, z, c)))
        peers.append((y, block_of(x, (z + d) % 4, c)))
        peers.append(((y + d) % 4, b))
    for peer in peers:
        pl.semaphore_signal(barrier, inc=1, device_id=peer, device_id_type=MESH)
    pl.semaphore_wait(barrier, len(peers))

    halo = []
    for n, (src, dst) in enumerate(((u_hbm, hu), (l_hbm, hl), (k_hbm, hk))):

        def rows(r):
            return src.at[:, 0, pl.ds(r, 8), :] if len(src.shape) == 4 else src.at[0, pl.ds(r, 8), :]

        halo.append(remote(rows(120), dst.at[0], halo_s.at[n], halo_r.at[n], y, nxt))
        halo.append(remote(rows(0), dst.at[1], halo_s.at[3 + n], halo_r.at[3 + n], y, prv))
    for copy in halo:
        copy.start()

    for copy in loads[3] + maps:
        copy.wait()
    for v in range(V):
        chunk[KU * v : KU * (v + 1), :] = u0[v, 3, 16:144, :].T[128 - KU :, :]
        chunk[OFF_L + KL * v : OFF_L + KL * (v + 1), :] = l4[v, 3, 16:144, :].T[128 - KL :, :]
    chunk[OFF_K : OFF_K + KU, :] = kap[3, 16:144, :].T[128 - KU :, :]
    chunk[OFF_M : OFF_M + 4, :] = mt[...].astype(F32)
    chunk[OFF_W : OFF_W + 4, :] = wt[...]

    here = gat.at[q, x, z * 2 + c]
    across = remote(chunk, here, first_s.at[0], first_r.at[c], yp, b0 + q)
    across.start()

    @pl.when(c == q)
    def _():
        gat[q, x, z * 2 + c] = chunk[...]

    @pl.when(c != q)
    def _():
        remote(chunk, here, first_s.at[1], first_r.at[2], y, b0 + q).start()

    def part(core, stage, d):
        if core == 0:
            if stage == 0:
                return gat.at[0, (x + d) % 4, pl.ds(z * 2, 2)]
            return gat.at[0, :, pl.ds((z + d) % 4 * 2, 2)]
        if stage == 0:
            return gat.at[1, x, pl.ds((z + d) % 4 * 2, 2)]
        return gat.at[1, (x + d) % 4]

    def hops(core, stage):
        copies = []
        for d in (1, 2, 3):
            to = block_of((x + d) % 4, z, c) if core == stage else block_of(x, (z + d) % 4, c)
            n = 3 * stage + d - 1
            copies.append(remote(part(core, stage, 0), part(core, stage, 0), ph_s.at[n], ph_r.at[n], y, to))
        return copies

    def swaps(core, whose):
        return [
            remote(part(whose, 1, d), part(whose, 1, d), core_s.at[d], core_r.at[d], y, twin) for d in range(4)
        ]

    def on_core(core, action):
        @pl.when(c == core)
        def _():
            action(core)

    def first_stage(core):
        @pl.when(q == core)
        def _():
            remote(chunk, here, first_s.at[1], first_r.at[2], y, b0 + q).wait_recv()

        @pl.when(q != core)
        def _():
            for j in range(2):
                remote(chunk, here, first_s.at[0], first_r.at[j], yp, b0 + q).wait_recv()

        for copy in hops(core, 0):
            copy.start()

    def second_stage(core):
        for copy in hops(core, 0):
            copy.wait()
        for copy in hops(core, 1):
            copy.start()
        swaps(core, core)[0].start()

    def third_stage(core):
        copies, sends = hops(core, 1), swaps(core, core)
        for copy in copies:
            copy.wait()
        for copy in sends[1:]:
            copy.start()

    def last_stage(core):
        for copy in swaps(core, core):
            copy.wait_send()
        for copy in swaps(core, 1 - core):
            copy.wait_recv()

    for core in range(2):
        on_core(core, first_stage)

    for copy in halo:
        copy.wait()
    for copy in loads[0] + loads[1] + loads[2]:
        copy.wait()
    for t in range(4):
        cut = slice(t * 128, (t + 1) * 128)
        for side, r in ((0, 8), (1, 144)):
            kap[t, r : r + 8, :] = hk[side, :, cut]
            for v in range(V):
                u0[v, t, r : r + 8, :] = hu[side, v, :, cut]
                l4[v, t, r : r + 8, :] = hl[side, v, :, cut]

    def scale(i):
        rows = pl.ds(pl.multiple_of(8 + i * 8, 8), 8)
        for t in range(4):
            k = kap[t, rows, :]
            for v in range(V):
                s4[v, t, rows, :] = k * l4[v, t, rows, :]

    over_rows(scale, 0, 18, 2)
    for core in range(2):
        on_core(core, second_stage)

    every = (0, 1, 2, 3)
    for n in range(3):
        main_forward(n, us, ds, kap, coup, every, None)
    for n in (3, 2, 1, 0):
        main_adjoint(n, us, ds, ls, ss, kap, coup, every, None, hsum, outv)

    for core in range(2):
        on_core(core, third_stage)

    scatter_points(hsum, area, proj, ids, dist, partial)
    first = remote(
        partial.at[:, pl.ds(pl.multiple_of((1 - c) * 64, 64), 64), :], r1, rs_s.at[0], rs_r.at[0], y, twin
    )
    first.start()
    for core in range(2):
        on_core(core, last_stage)
    across.wait_send()

    @pl.when(c != q)
    def _():
        remote(chunk, here, first_s.at[1], first_r.at[2], y, b0 + q).wait_send()

    def sent(slots, got, base, to_of):
        copies = []
        for d in (1, 2, 3):
            index, ty, tb = to_of(d)
            copies.append(
                remote(slots.at[index], got.at[d - 1], rs_s.at[base + d], rs_r.at[base + d], ty, tb)
            )
        return copies

    by_x = sent(q1, r2, 0, lambda d: ((x + d) % 4, y, block_of((x + d) % 4, z, c)))
    by_z = sent(q2, r3, 3, lambda d: ((z + d) % 4, y, block_of(x, (z + d) % 4, c)))
    by_y = sent(q3, r4, 6, lambda d: ((y + d) % 4, (y + d) % 4, b))

    def between(step):
        if step == 0:
            first.wait()
            own = pl.multiple_of(c * 64, 64)
            for j in range(4):
                q1[j] = partial[:, pl.ds(own + j * 16, 16), :] + r1[:, j * 16 : (j + 1) * 16, :]
            for copy in by_x:
                copy.start()
        if step == 2:
            for copy in by_x:
                copy.wait()
            total = q1[x] + r2[0] + r2[1] + r2[2]
            for j in range(4):
                q2[j] = total[:, j * 4 : (j + 1) * 4, :]
            for copy in by_z:
                copy.start()
        if step == 4:
            for copy in by_z:
                copy.wait()
            total = q2[z] + r3[0] + r3[1] + r3[2]
            for j in range(4):
                q3[j] = total[:, j, :]
            for copy in by_y:
                copy.start()

    strips(gat.reshape(2, 32 * CHUNK, 128), q, coup, su, sd, sl, sk, tap, shift, ring, tring, face, between)
    for copy in by_y:
        copy.wait()
    points[...] = q3[y] + r4[0] + r4[1] + r4[2]

    face_columns(face.reshape(2, 35 * 32, 128), q, b, cols)
    stores = [
        pltpu.make_async_copy(outv.at[:, t], out_hbm.at[:, 0, :, pl.ds(t * 128, 128)], osem.at[t])
        for t in range(4)
    ]
    for copy in stores[:3]:
        copy.start()
    for n in range(3):
        main_forward(n, us, ds, kap, coup, (3,), cols)
    for n in (3, 2, 1, 0):
        main_adjoint(n, us, ds, ls, ss, kap, coup, (3,), cols, None, outv)
    stores[3].start()
    for copy in stores:
        copy.wait()


def local(
    start_state, diffusivity, donor_map, donor_weight, coupling, final_cotangent,
    wall_area, wall_projection, center_ids, center_dist,
):
    any_ = pl.BlockSpec(memory_space=pl.ANY)
    vmem = pl.BlockSpec(memory_space=pltpu.VMEM)
    smem = pl.BlockSpec(memory_space=pltpu.SMEM)
    dma = pltpu.SemaphoreType.DMA

    def buf(*shape, dtype=F32):
        return pltpu.VMEM(shape, dtype)

    return pl.pallas_call(
        window_kernel,
        out_shape=(jax.ShapeDtypeStruct((V, 1, 128, 512), F32), jax.ShapeDtypeStruct((3, 256), F32)),
        in_specs=[smem, smem, any_, any_, any_, any_, any_, vmem, vmem, vmem],
        out_specs=(any_, vmem),
        scratch_shapes=[buf(V, 4, ROWS, 128)] * 15
        + [
            buf(4, ROWS, 128),
            buf(V, ROWS, 128),
            buf(V, 4, 128, 128),
            buf(4, 2, V, KU, 32, 128),
            buf(3, 2, V, 2, 32, 128),
            buf(4, 2, V, KL, 32, 128),
            buf(2, KU, 32, 128),
            buf(2, 4, 6, 32, 128),
            buf(2, V, 72, 128),
            buf(72, 128),
            buf(2, 35, 32, 128),
            buf(ROWS, 128),
            pltpu.SMEM((2, 4), jnp.int32),
            buf(2, 4, 8, CHUNK, 128),
            buf(2, V, 8, 512),
            buf(2, V, 8, 512),
            buf(2, 8, 512),
            buf(CHUNK, 128),
            buf(4, 128, dtype=jnp.int32),
            buf(4, 128),
            buf(3, 128, 256),
            buf(3, 64, 256),
            buf(4, 3, 16, 256),
            buf(3, 3, 16, 256),
            buf(4, 3, 4, 256),
            buf(3, 3, 4, 256),
            buf(4, 3, 256),
            buf(3, 3, 256),
        ]
        + [dma((n,)) for n in (14, 4, 6, 6, 2, 3, 6, 6, 4, 4, 10, 10)],
        compiler_params=pltpu.CompilerParams(
            collective_id=0, has_side_effects=True, vmem_limit_bytes=60 * 1024 * 1024
        ),
        name="window",
    )(
        coupling, wall_projection, start_state, diffusivity, final_cotangent, donor_map, donor_weight,
        wall_area, center_ids[0], center_dist[0],
    )


def solution(mesh):
    return jax.shard_map(
        local,
        mesh=mesh,
        in_specs=(
            P(None, "zone", "block", None),
            P("zone", "block", None),
            P(None, "zone", None),
            P(None, "zone", None),
            P(),
            P(None, "zone", "block", None),
            P("zone", "block"),
            P(),
            P("zone", None, "block"),
            P("zone", None, "block"),
        ),
        out_specs=(P(None, "zone", "block", None), P(None, ("zone", "block"))),
        check_vma=False,
    )
```

time: 91.6 us -> 57.1 us (0.62)
  the two profiles are of different devices: /device:TPU:1 before, /device:TPU:0 now
where the time goes in v2:
time: 57.1 us; the launch traced here: 56.9 us
  Pallas kernels  53.2 us (93%)
  local copies, waits for them, and re-layouts  3.12 us (5%)
  between operations  0.65 us (1%)
    pallas_call x1, Pallas kernels, local(): pl.pallas_call(window_kernel, out_shape=(jax.ShapeDtypeStruct((V, 1, 128,...  53.2 us
    unnamed x4, local copies, waits for them, and re-layouts  3.12 us

profile of v2, /device:TPU:0, one launch (start us, length us, event | category | flops | bytes accessed | tf_op | source)
XLA Modules:
  0.0 56.9 jit_solution(2540988557000282521)
XLA Ops:
  0.6 53.2 %window.1 = (f32[5,1,128,512]{3,2,1,0:T(8,128)}, f32[3,256]{1,0:T(4,128)}) custom-call(f32[5,5]{1,0:T(8,128)} %coup.1, f32[3,5]{1,0:T(4,128)} %proj.1, f32[5,1,128,512]{3,2,1,0:T(8,128)} %u_hbm.1, f32[1,128,512]{2,1,0:T(8,128)} %k_hbm.1, f32[5,1,128,512]{3,2,1,0:T(8,128)} %l_hbm.1, s32[4,1,4096]{2,1,0:T(1,128)} %m_hbm.1, f32[4,1,4096]{2,1,0:T(1,128)} %w_hbm.1, ...), custom_call_target="tpu_custom_call" | custom-call | tf_op jit(solution)/shard_map/window/pallas_call | solution.py:587
  53.8 0.0 copy-start
  53.8 2.5 %copy.14 = f32[5,1,128,512]{3,2,1,0:T(8,128)} copy(f32[5,1,128,512]{3,2,1,0:T(8,128)} %get-tuple-element.4) | data formatting | bytes 2621440
  56.4 0.0 copy-done
  56.4 0.6 %copy.15 = f32[3,256]{1,0:T(4,128)} copy(f32[3,256]{1,0:T(4,128)S(1)} %copy-done) | data formatting | bytes 6144
Async XLA Ops:
  53.8 2.5 %copy-start = (f32[3,256]{1,0:T(4,128)S(1)}, f32[3,256]{1,0:T(4,128)}, u32[]{:S(2)}) copy-start(f32[3,256]{1,0:T(4,128)} %get-tuple-element.5) | copy-start | bytes 9220

commit v3 on v2

--- a/solution.py
+++ b/solution.py
@@ -49,7 +49,16 @@
     lax.fori_loop(0, count // unroll, several, 0)
 
 
-def main_forward(n, us, ds, kap, coup, tiles, ghost):
+def over_edges(body, count):
+    def side(i, carry):
+        for j in range(count):
+            body(i * (18 - count) + j)
+        return carry
+
+    lax.fori_loop(0, 2, side, 0)
+
+
+def main_forward(n, us, ds, kap, kc, coup, tiles, ghost, where):
     lane = lane_of((8, 128))
     cf = [[coup[v, w] for w in range(V)] for v in range(V)]
     src, dst, dd = us[n], us[n + 1], ds[n]
@@ -59,8 +68,9 @@
         rows = pl.ds(r, 8)
         for t in tiles:
             k = kap[t, rows, :]
+            a = kc[t, rows, :]
             cur = [src[v, t, rows, :] for v in range(V)]
-            th = [jnp.tanh(a) for a in cur]
+            th = [jnp.tanh(e) for e in cur]
             for v in range(V):
                 if t == 0:
                     left = jnp.where(lane == 127, 0.0, cur[v])
@@ -75,18 +85,30 @@
                     right = jnp.where(lane == 0, g, cur[v])
                 lap = (
                     src[v, t, pl.ds(r - 1, 8), :] + src[v, t, pl.ds(r + 1, 8), :]
-                    + pltpu.roll(left, 1, 1) + pltpu.roll(right, 127, 1) - 4.0 * cur[v]
+                    + pltpu.roll(left, 1, 1) + pltpu.roll(right, 127, 1)
                 )
                 react = cf[v][0] * th[0]
                 for w in range(1, V):
                     react = react + cf[v][w] * th[w]
-                dst[v, t, rows, :] = cur[v] + k * lap - react
+                dst[v, t, rows, :] = a * cur[v] + k * lap - react
                 dd[v, t, rows, :] = 1.0 - th[v] * th[v]
 
-    over_rows(body, 0, 18, 6 if len(tiles) == 1 else 2)
-
-
-def main_adjoint(n, us, ds, ls, ss, kap, coup, tiles, back, hsum, out):
+    where(body)
+
+
+def inner(margin):
+    return lambda body: over_rows(body, margin, 18 - 2 * margin, 2)
+
+
+def edges(count):
+    return lambda body: over_edges(body, count)
+
+
+def all_rows(body):
+    over_rows(body, 0, 18, 6)
+
+
+def main_adjoint(n, us, ds, ls, ss, kap, kc, coup, tiles, back, hsum, out):
     lane = lane_of((8, 128))
     cf = [[coup[w, v] for w in range(V)] for v in range(V)]
     m = 3 - n
@@ -97,6 +119,7 @@
         rows = pl.ds(r, 8)
         for t in tiles:
             cur = [lam[v, t, rows, :] for v in range(V)]
+            a = kc[t, rows, :]
             for v in range(V):
                 s = sca[v, t, rows, :]
                 if t == 0:
@@ -106,7 +129,7 @@
                 right = jnp.where(lane == 0, sca[v, t + 1, rows, :] if t < 3 else 0.0, s)
                 lap = (
                     sca[v, t, pl.ds(r - 1, 8), :] + sca[v, t, pl.ds(r + 1, 8), :]
-                    + pltpu.roll(left, 1, 1) + pltpu.roll(right, 127, 1) - 4.0 * s
+                    + pltpu.roll(left, 1, 1) + pltpu.roll(right, 127, 1)
                 )
                 if n == 3:
                     th = jnp.tanh(us[3][v, t, rows, :])
@@ -116,7 +139,7 @@
                 pulled = cf[v][0] * cur[0]
                 for w in range(1, V):
                     pulled = pulled + cf[v][w] * cur[w]
-                new = cur[v] + lap - d * pulled
+                new = a * cur[v] + lap - d * pulled
                 if t == 3 and back is not None:
                     f = pltpu.roll(back[rows, :], 127 - (15 + n * V + v), 1)
                     new = new + jnp.where(lane == 127, f, 0.0)
@@ -159,7 +182,7 @@
     return pltpu.roll(jnp.where(lane < low, second, first), (128 - low) % 128, 1)
 
 
-def strips(gat, q, coup, su, sd, sl, sk, tap, shift, ring, tring, face, between):
+def strips(gat, q, coup, su, sd, sl, sk, tap, shift, ring, tring, face):
     row = lax.broadcasted_iota(jnp.int32, (32, 128), 0) * 128 + lane_of((32, 128))
 
     def get(zone, j):
@@ -224,7 +247,6 @@
             return carry
 
         lax.fori_loop(0, 2, step, 0)
-        between(n)
 
     for n in (3, 2, 1, 0):
         m = 3 - n
@@ -273,7 +295,6 @@
             lax.fori_loop(0, 2, back, 0)
         else:
             back(q, 0)
-        between(6 - n)
 
 
 def face_columns(face, q, b, cols):
@@ -283,9 +304,9 @@
         cols[dst : dst + size, :] = jnp.concatenate([rows, pad], axis=0).T[lo : lo + size, :]
 
 
-def scatter_points(hsum, area, proj, ids, dist, partial):
+def scatter_points(hsum, l1, u0, area, proj, ids, dist, partial):
     lane = lane_of((128, 128))
-    hs = [hsum[v, 16:144, :] for v in range(V)]
+    hs = [hsum[v, 16:144, :] + l1[v, 0, 16:144, :] * u0[v, 0, 16:144, :] for v in range(V)]
     acc = jnp.zeros((128, 128), F32)
     for c in range(3):
         col = proj[c, 0] * hs[0]
@@ -332,7 +353,7 @@
 
 def window_kernel(
     coup, proj, u_hbm, k_hbm, l_hbm, m_hbm, w_hbm, area, ids, dist, out_hbm, points,
-    u0, u1, u2, u3, d0, d1, d2, l4, l3, l2, l1, s4, s3, s2, s1, kap, hsum, outv,
+    u0, u1, u2, u3, d0, d1, d2, l4, l3, l2, l1, s4, s3, s2, s1, kap, kc, hsum, outv,
     su, sd, sl, sk, tap, ring, tring, face, cols, shift,
     gat, hu, hl, hk, chunk, mt, wt, partial, r1, q1, r2, q2, r3, q3, r4,
     sem, osem, halo_s, halo_r, first_s, first_r, ph_s, ph_r, core_s, core_r, rs_s, rs_r,
@@ -371,7 +392,6 @@
         peers.append(((y + d) % 4, b))
     for peer in peers:
         pl.semaphore_signal(barrier, inc=1, device_id=peer, device_id_type=MESH)
-    pl.semaphore_wait(barrier, len(peers))
 
     halo = []
     for n, (src, dst) in enumerate(((u_hbm, hu), (l_hbm, hl), (k_hbm, hk))):
@@ -381,8 +401,6 @@
 
         halo.append(remote(rows(120), dst.at[0], halo_s.at[n], halo_r.at[n], y, nxt))
         halo.append(remote(rows(0), dst.at[1], halo_s.at[3 + n], halo_r.at[3 + n], y, prv))
-    for copy in halo:
-        copy.start()
 
     for copy in loads[3] + maps:
         copy.wait()
@@ -393,9 +411,27 @@
     chunk[OFF_M : OFF_M + 4, :] = mt[...].astype(F32)
     chunk[OFF_W : OFF_W + 4, :] = wt[...]
 
+    for copy in loads[0] + loads[1] + loads[2]:
+        copy.wait()
+
+    def scale(i):
+        rows = pl.ds(pl.multiple_of(8 + i * 8, 8), 8)
+        for t in range(4):
+            k = kap[t, rows, :]
+            kc[t, rows, :] = 1.0 - 4.0 * k
+            for v in range(V):
+                s4[v, t, rows, :] = k * l4[v, t, rows, :]
+
+    every = (0, 1, 2, 3)
+    over_rows(scale, 1, 16, 2)
+    main_forward(0, us, ds, kap, kc, coup, every, None, inner(2))
+    pl.semaphore_wait(barrier, len(peers))
+
     here = gat.at[q, x, z * 2 + c]
     across = remote(chunk, here, first_s.at[0], first_r.at[c], yp, b0 + q)
     across.start()
+    for copy in halo:
+        copy.start()
 
     @pl.when(c == q)
     def _():
@@ -465,12 +501,12 @@
         for copy in swaps(core, 1 - core):
             copy.wait_recv()
 
+    main_forward(1, us, ds, kap, kc, coup, every, None, inner(3))
     for core in range(2):
         on_core(core, first_stage)
+    main_forward(2, us, ds, kap, kc, coup, every, None, inner(4))
 
     for copy in halo:
-        copy.wait()
-    for copy in loads[0] + loads[1] + loads[2]:
         copy.wait()
     for t in range(4):
         cut = slice(t * 128, (t + 1) * 128)
@@ -480,38 +516,19 @@
                 u0[v, t, r : r + 8, :] = hu[side, v, :, cut]
                 l4[v, t, r : r + 8, :] = hl[side, v, :, cut]
 
-    def scale(i):
-        rows = pl.ds(pl.multiple_of(8 + i * 8, 8), 8)
-        for t in range(4):
-            k = kap[t, rows, :]
-            for v in range(V):
-                s4[v, t, rows, :] = k * l4[v, t, rows, :]
-
-    over_rows(scale, 0, 18, 2)
+    over_edges(scale, 1)
+    for n in range(3):
+        main_forward(n, us, ds, kap, kc, coup, every, None, edges(n + 2))
     for core in range(2):
         on_core(core, second_stage)
 
-    every = (0, 1, 2, 3)
-    for n in range(3):
-        main_forward(n, us, ds, kap, coup, every, None)
-    for n in (3, 2, 1, 0):
-        main_adjoint(n, us, ds, ls, ss, kap, coup, every, None, hsum, outv)
-
-    for core in range(2):
-        on_core(core, third_stage)
-
-    scatter_points(hsum, area, proj, ids, dist, partial)
+    for n in (3, 2, 1):
+        main_adjoint(n, us, ds, ls, ss, kap, kc, coup, (0,), None, hsum, outv)
+    scatter_points(hsum, l1, u0, area, proj, ids, dist, partial)
     first = remote(
         partial.at[:, pl.ds(pl.multiple_of((1 - c) * 64, 64), 64), :], r1, rs_s.at[0], rs_r.at[0], y, twin
     )
     first.start()
-    for core in range(2):
-        on_core(core, last_stage)
-    across.wait_send()
-
-    @pl.when(c != q)
-    def _():
-        remote(chunk, here, first_s.at[1], first_r.at[2], y, b0 + q).wait_send()
 
     def sent(slots, got, base, to_of):
         copies = []
@@ -526,7 +543,7 @@
     by_z = sent(q2, r3, 3, lambda d: ((z + d) % 4, y, block_of(x, (z + d) % 4, c)))
     by_y = sent(q3, r4, 6, lambda d: ((y + d) % 4, (y + d) % 4, b))
 
-    def between(step):
+    def reduce_stage(step):
         if step == 0:
             first.wait()
             own = pl.multiple_of(c * 64, 64)
@@ -534,7 +551,7 @@
                 q1[j] = partial[:, pl.ds(own + j * 16, 16), :] + r1[:, j * 16 : (j + 1) * 16, :]
             for copy in by_x:
                 copy.start()
-        if step == 2:
+        if step == 1:
             for copy in by_x:
                 copy.wait()
             total = q1[x] + r2[0] + r2[1] + r2[2]
@@ -542,7 +559,7 @@
                 q2[j] = total[:, j * 4 : (j + 1) * 4, :]
             for copy in by_z:
                 copy.start()
-        if step == 4:
+        if step == 2:
             for copy in by_z:
                 copy.wait()
             total = q2[z] + r3[0] + r3[1] + r3[2]
@@ -550,12 +567,26 @@
                 q3[j] = total[:, j, :]
             for copy in by_y:
                 copy.start()
-
-    strips(gat.reshape(2, 32 * CHUNK, 128), q, coup, su, sd, sl, sk, tap, shift, ring, tring, face, between)
-    for copy in by_y:
-        copy.wait()
-    points[...] = q3[y] + r4[0] + r4[1] + r4[2]
-
+        if step == 3:
+            for copy in by_y:
+                copy.wait()
+            points[...] = q3[y] + r4[0] + r4[1] + r4[2]
+
+    for n in (3, 2, 1, 0):
+        main_adjoint(n, us, ds, ls, ss, kap, kc, coup, every, None, None, outv)
+        reduce_stage(3 - n)
+        if n == 2:
+            for core in range(2):
+                on_core(core, third_stage)
+    for core in range(2):
+        on_core(core, last_stage)
+    across.wait_send()
+
+    @pl.when(c != q)
+    def _():
+        remote(chunk, here, first_s.at[1], first_r.at[2], y, b0 + q).wait_send()
+
+    strips(gat.reshape(2, 32 * CHUNK, 128), q, coup, su, sd, sl, sk, tap, shift, ring, tring, face)
     face_columns(face.reshape(2, 35 * 32, 128), q, b, cols)
     stores = [
         pltpu.make_async_copy(outv.at[:, t], out_hbm.at[:, 0, :, pl.ds(t * 128, 128)], osem.at[t])
@@ -564,9 +595,9 @@
     for copy in stores[:3]:
         copy.start()
     for n in range(3):
-        main_forward(n, us, ds, kap, coup, (3,), cols)
+        main_forward(n, us, ds, kap, kc, coup, (3,), cols, all_rows)
     for n in (3, 2, 1, 0):
-        main_adjoint(n, us, ds, ls, ss, kap, coup, (3,), cols, None, outv)
+        main_adjoint(n, us, ds, ls, ss, kap, kc, coup, (3,), cols, None, outv)
     stores[3].start()
     for copy in stores:
         copy.wait()
@@ -591,6 +622,7 @@
         out_specs=(any_, vmem),
         scratch_shapes=[buf(V, 4, ROWS, 128)] * 15
         + [
+            buf(4, ROWS, 128),
             buf(4, ROWS, 128),
             buf(V, ROWS, 128),
             buf(V, 4, 128, 128),

time: 57.1 us -> 51.8 us (0.907)
  the two profiles are of different devices: /device:TPU:0 before, /device:TPU:1 now
where the time goes in v3:
time: 51.8 us; the launch traced here: 51 us
  Pallas kernels  47.2 us (91%)
  local copies, waits for them, and re-layouts  3.12 us (6%)
  between operations  0.65 us (1%)
    pallas_call x1, Pallas kernels, local(): pl.pallas_call(window_kernel, out_shape=(jax.ShapeDtypeStruct((V, 1, 128,...  47.2 us
    unnamed x4, local copies, waits for them, and re-layouts  3.12 us

profile of v3, /device:TPU:1, one launch (start us, length us, event | category | flops | bytes accessed | tf_op | source)
XLA Modules:
  0.0 51.0 jit_solution(17743009726026224882)
XLA Ops:
  0.6 47.2 %window.1 = (f32[5,1,128,512]{3,2,1,0:T(8,128)}, f32[3,256]{1,0:T(4,128)}) custom-call(f32[5,5]{1,0:T(8,128)} %coup.1, f32[3,5]{1,0:T(4,128)} %proj.1, f32[5,1,128,512]{3,2,1,0:T(8,128)} %u_hbm.1, f32[1,128,512]{2,1,0:T(8,128)} %k_hbm.1, f32[5,1,128,512]{3,2,1,0:T(8,128)} %l_hbm.1, s32[4,1,4096]{2,1,0:T(1,128)} %m_hbm.1, f32[4,1,4096]{2,1,0:T(1,128)} %w_hbm.1, ...), custom_call_target="tpu_custom_call" | custom-call | tf_op jit(solution)/shard_map/window/pallas_call | solution.py:618
  47.9 0.0 copy-start
  47.9 2.5 %copy.14 = f32[5,1,128,512]{3,2,1,0:T(8,128)} copy(f32[5,1,128,512]{3,2,1,0:T(8,128)} %get-tuple-element.4) | data formatting | bytes 2621440
  50.4 0.0 copy-done
  50.4 0.6 %copy.15 = f32[3,256]{1,0:T(4,128)} copy(f32[3,256]{1,0:T(4,128)S(1)} %copy-done) | data formatting | bytes 6144
Async XLA Ops:
  47.9 2.5 %copy-start = (f32[3,256]{1,0:T(4,128)S(1)}, f32[3,256]{1,0:T(4,128)}, u32[]{:S(2)}) copy-start(f32[3,256]{1,0:T(4,128)} %get-tuple-element.5) | copy-start | bytes 9220

commit v4 on v3

--- a/solution.py
+++ b/solution.py
@@ -182,7 +182,7 @@
     return pltpu.roll(jnp.where(lane < low, second, first), (128 - low) % 128, 1)
 
 
-def strips(gat, q, coup, su, sd, sl, sk, tap, shift, ring, tring, face):
+def strips(gat, q, coup, su, sd, sl, sk, tap, shift, ring, tring, face, between):
     row = lax.broadcasted_iota(jnp.int32, (32, 128), 0) * 128 + lane_of((32, 128))
 
     def get(zone, j):
@@ -247,6 +247,7 @@
             return carry
 
         lax.fori_loop(0, 2, step, 0)
+        between(n)
 
     for n in (3, 2, 1, 0):
         m = 3 - n
@@ -574,8 +575,8 @@
 
     for n in (3, 2, 1, 0):
         main_adjoint(n, us, ds, ls, ss, kap, kc, coup, every, None, None, outv)
-        reduce_stage(3 - n)
         if n == 2:
+            reduce_stage(0)
             for core in range(2):
                 on_core(core, third_stage)
     for core in range(2):
@@ -586,7 +587,14 @@
     def _():
         remote(chunk, here, first_s.at[1], first_r.at[2], y, b0 + q).wait_send()
 
-    strips(gat.reshape(2, 32 * CHUNK, 128), q, coup, su, sd, sl, sk, tap, shift, ring, tring, face)
+    reduce_stage(1)
+
+    def between(n):
+        if n == 1:
+            reduce_stage(2)
+
+    strips(gat.reshape(2, 32 * CHUNK, 128), q, coup, su, sd, sl, sk, tap, shift, ring, tring, face, between)
+    reduce_stage(3)
     face_columns(face.reshape(2, 35 * 32, 128), q, b, cols)
     stores = [
         pltpu.make_async_copy(outv.at[:, t], out_hbm.at[:, 0, :, pl.ds(t * 128, 128)], osem.at[t])

time: 51.8 us -> 46.5 us (0.90)
  Pallas kernels: 47.2 us -> 41.8 us
    pallas_call x1, Pallas kernels: 47.2 us -> 41.8 us  [local(): pl.pallas_call(window_kernel, out_shape=(jax.ShapeDtypeStruct((V, 1, 128,...]
where the time goes in v4:
time: 46.5 us; the launch traced here: 45.5 us
  Pallas kernels  41.8 us (90%)
  local copies, waits for them, and re-layouts  3.12 us (7%)
  between operations  0.65 us (1%)
    pallas_call x1, Pallas kernels, local(): pl.pallas_call(window_kernel, out_shape=(jax.ShapeDtypeStruct((V, 1, 128,...  41.8 us
    unnamed x4, local copies, waits for them, and re-layouts  3.12 us

profile of v4, /device:TPU:1, one launch (start us, length us, event | category | flops | bytes accessed | tf_op | source)
XLA Modules:
  0.0 45.5 jit_solution(18255613319464338405)
XLA Ops:
  0.6 41.8 %window.1 = (f32[5,1,128,512]{3,2,1,0:T(8,128)}, f32[3,256]{1,0:T(4,128)}) custom-call(f32[5,5]{1,0:T(8,128)} %coup.1, f32[3,5]{1,0:T(4,128)} %proj.1, f32[5,1,128,512]{3,2,1,0:T(8,128)} %u_hbm.1, f32[1,128,512]{2,1,0:T(8,128)} %k_hbm.1, f32[5,1,128,512]{3,2,1,0:T(8,128)} %l_hbm.1, s32[4,1,4096]{2,1,0:T(1,128)} %m_hbm.1, f32[4,1,4096]{2,1,0:T(1,128)} %w_hbm.1, ...), custom_call_target="tpu_custom_call" | custom-call | tf_op jit(solution)/shard_map/window/pallas_call | solution.py:626
  42.4 0.0 copy-start
  42.4 2.5 %copy.14 = f32[5,1,128,512]{3,2,1,0:T(8,128)} copy(f32[5,1,128,512]{3,2,1,0:T(8,128)} %get-tuple-element.4) | data formatting | bytes 2621440
  44.9 0.0 copy-done
  44.9 0.6 %copy.15 = f32[3,256]{1,0:T(4,128)} copy(f32[3,256]{1,0:T(4,128)S(1)} %copy-done) | data formatting | bytes 6144
Async XLA Ops:
  42.4 2.5 %copy-start = (f32[3,256]{1,0:T(4,128)S(1)}, f32[3,256]{1,0:T(4,128)}, u32[]{:S(2)}) copy-start(f32[3,256]{1,0:T(4,128)} %get-tuple-element.5) | copy-start | bytes 9220

commit v5 on v4

--- a/solution.py
+++ b/solution.py
@@ -108,7 +108,7 @@
     over_rows(body, 0, 18, 6)
 
 
-def main_adjoint(n, us, ds, ls, ss, kap, kc, coup, tiles, back, hsum, out):
+def main_adjoint(n, us, ds, ls, ss, kap, kc, coup, tiles, back, hsum, out, where=None):
     lane = lane_of((8, 128))
     cf = [[coup[w, v] for w in range(V)] for v in range(V)]
     m = 3 - n
@@ -155,7 +155,9 @@
                     else:
                         hsum[v, rows, :] = hsum[v, rows, :] + p
 
-    if n > 0:
+    if where is not None:
+        where(body)
+    elif n > 0:
         over_rows(body, 0, 18, 6 if len(tiles) == 1 else 2)
     else:
         over_rows(body, 1, 16, 4 if len(tiles) == 1 else 2)
@@ -182,13 +184,18 @@
     return pltpu.roll(jnp.where(lane < low, second, first), (128 - low) % 128, 1)
 
 
-def strips(gat, q, coup, su, sd, sl, sk, tap, shift, ring, tring, face, between):
+def strips(gat, q, coup, su, sd, sl, sk, tap, shift, ring, tring, face, turned, between):
     row = lax.broadcasted_iota(jnp.int32, (32, 128), 0) * 128 + lane_of((32, 128))
 
     def get(zone, j):
-        return gat[zone, pl.ds(j, 32, stride=CHUNK), :]
+        return turned[j]
 
     def unpack(zone, carry):
+        for j in range(CHUNK // 8):
+            for i in range(4):
+                turned[j * 8 : (j + 1) * 8, i * 8 : (i + 1) * 8, :] = jnp.swapaxes(
+                    gat[zone, i, :, j * 8 : (j + 1) * 8, :], 0, 1
+                )
         for v in range(V):
             for k in range(KU):
                 su[0, zone, v, k] = get(zone, v * KU + KU - 1 - k)
@@ -356,7 +363,7 @@
     coup, proj, u_hbm, k_hbm, l_hbm, m_hbm, w_hbm, area, ids, dist, out_hbm, points,
     u0, u1, u2, u3, d0, d1, d2, l4, l3, l2, l1, s4, s3, s2, s1, kap, kc, hsum, outv,
     su, sd, sl, sk, tap, ring, tring, face, cols, shift,
-    gat, hu, hl, hk, chunk, mt, wt, partial, r1, q1, r2, q2, r3, q3, r4,
+    gat, hu, hl, hk, chunk, mt, wt, partial, r1, q1, r2, q2, r3, q3, r4, turned,
     sem, osem, halo_s, halo_r, first_s, first_r, ph_s, ph_r, core_s, core_r, rs_s, rs_r,
 ):
     y, b, x, z, c = place()
@@ -506,6 +513,9 @@
     for core in range(2):
         on_core(core, first_stage)
     main_forward(2, us, ds, kap, kc, coup, every, None, inner(4))
+
+    for n in (3, 2, 1):
+        main_adjoint(n, us, ds, ls, ss, kap, kc, coup, every, None, None, outv, inner(8 - n))
 
     for copy in halo:
         copy.wait()
@@ -574,7 +584,8 @@
             points[...] = q3[y] + r4[0] + r4[1] + r4[2]
 
     for n in (3, 2, 1, 0):
-        main_adjoint(n, us, ds, ls, ss, kap, kc, coup, every, None, None, outv)
+        rest = None if n == 0 else edges(8 - n)
+        main_adjoint(n, us, ds, ls, ss, kap, kc, coup, every, None, None, outv, rest)
         if n == 2:
             reduce_stage(0)
             for core in range(2):
@@ -587,14 +598,14 @@
     def _():
         remote(chunk, here, first_s.at[1], first_r.at[2], y, b0 + q).wait_send()
 
-    reduce_stage(1)
 
     def between(n):
-        if n == 1:
+        if n == 0:
+            reduce_stage(1)
+        if n == 2:
             reduce_stage(2)
 
-    strips(gat.reshape(2, 32 * CHUNK, 128), q, coup, su, sd, sl, sk, tap, shift, ring, tring, face, between)
-    reduce_stage(3)
+    strips(gat, q, coup, su, sd, sl, sk, tap, shift, ring, tring, face, turned, between)
     face_columns(face.reshape(2, 35 * 32, 128), q, b, cols)
     stores = [
         pltpu.make_async_copy(outv.at[:, t], out_hbm.at[:, 0, :, pl.ds(t * 128, 128)], osem.at[t])
@@ -607,6 +618,7 @@
     for n in (3, 2, 1, 0):
         main_adjoint(n, us, ds, ls, ss, kap, kc, coup, (3,), cols, None, outv)
     stores[3].start()
+    reduce_stage(3)
     for copy in stores:
         copy.wait()
 
@@ -659,6 +671,7 @@
             buf(3, 3, 4, 256),
             buf(4, 3, 256),
             buf(3, 3, 256),
+            buf(CHUNK, 32, 128),
         ]
         + [dma((n,)) for n in (14, 4, 6, 6, 2, 3, 6, 6, 4, 4, 10, 10)],
         compiler_params=pltpu.CompilerParams(

time: 46.5 us -> 46.8 us (level); the launches traced: 45.5 us -> 46.6 us
  Pallas kernels: 41.8 us -> 42.8 us
    pallas_call x1, Pallas kernels: 41.8 us -> 42.8 us  [local(): pl.pallas_call(window_kernel, out_shape=(jax.ShapeDtypeStruct((V, 1, 128,...]
where the time goes in v5:
time: 46.8 us; the launch traced here: 46.6 us
  Pallas kernels  42.8 us (91%)
  local copies, waits for them, and re-layouts  3.12 us (7%)
  between operations  0.65 us (1%)
    pallas_call x1, Pallas kernels, local(): pl.pallas_call(window_kernel, out_shape=(jax.ShapeDtypeStruct((V, 1, 128,...  42.8 us
    unnamed x4, local copies, waits for them, and re-layouts  3.12 us

profile of v5, /device:TPU:1, one launch (start us, length us, event | category | flops | bytes accessed | tf_op | source)
XLA Modules:
  0.0 46.6 jit_solution(7360711244499541865)
XLA Ops:
  0.6 42.8 %window.1 = (f32[5,1,128,512]{3,2,1,0:T(8,128)}, f32[3,256]{1,0:T(4,128)}) custom-call(f32[5,5]{1,0:T(8,128)} %coup.1, f32[3,5]{1,0:T(4,128)} %proj.1, f32[5,1,128,512]{3,2,1,0:T(8,128)} %u_hbm.1, f32[1,128,512]{2,1,0:T(8,128)} %k_hbm.1, f32[5,1,128,512]{3,2,1,0:T(8,128)} %l_hbm.1, s32[4,1,4096]{2,1,0:T(1,128)} %m_hbm.1, f32[4,1,4096]{2,1,0:T(1,128)} %w_hbm.1, ...), custom_call_target="tpu_custom_call" | custom-call | tf_op jit(solution)/shard_map/window/pallas_call | solution.py:638
  43.5 0.0 copy-start
  43.5 2.5 %copy.14 = f32[5,1,128,512]{3,2,1,0:T(8,128)} copy(f32[5,1,128,512]{3,2,1,0:T(8,128)} %get-tuple-element.4) | data formatting | bytes 2621440
  46.0 0.0 copy-done
  46.0 0.6 %copy.15 = f32[3,256]{1,0:T(4,128)} copy(f32[3,256]{1,0:T(4,128)S(1)} %copy-done) | data formatting | bytes 6144
Async XLA Ops:
  43.5 2.5 %copy-start = (f32[3,256]{1,0:T(4,128)S(1)}, f32[3,256]{1,0:T(4,128)}, u32[]{:S(2)}) copy-start(f32[3,256]{1,0:T(4,128)} %get-tuple-element.5) | copy-start | bytes 9220

commit v6 on v5

--- a/solution.py
+++ b/solution.py
@@ -517,6 +517,9 @@
     for n in (3, 2, 1):
         main_adjoint(n, us, ds, ls, ss, kap, kc, coup, every, None, None, outv, inner(8 - n))
 
+    for core in range(2):
+        on_core(core, second_stage)
+
     for copy in halo:
         copy.wait()
     for t in range(4):
@@ -530,8 +533,6 @@
     over_edges(scale, 1)
     for n in range(3):
         main_forward(n, us, ds, kap, kc, coup, every, None, edges(n + 2))
-    for core in range(2):
-        on_core(core, second_stage)
 
     for n in (3, 2, 1):
         main_adjoint(n, us, ds, ls, ss, kap, kc, coup, (0,), None, hsum, outv)

time: 46.8 us -> 45.5 us (0.972)
  Pallas kernels: 42.8 us -> 41.5 us
    pallas_call x1, Pallas kernels: 42.8 us -> 41.5 us  [local(): pl.pallas_call(window_kernel, out_shape=(jax.ShapeDtypeStruct((V, 1, 128,...]
where the time goes in v6:
time: 45.5 us; the launch traced here: 45.2 us
  Pallas kernels  41.5 us (91%)
  local copies, waits for them, and re-layouts  3.12 us (7%)
  between operations  0.65 us (1%)
    pallas_call x1, Pallas kernels, local(): pl.pallas_call(window_kernel, out_shape=(jax.ShapeDtypeStruct((V, 1, 128,...  41.5 us
    unnamed x4, local copies, waits for them, and re-layouts  3.12 us

profile of v6, /device:TPU:1, one launch (start us, length us, event | category | flops | bytes accessed | tf_op | source)
XLA Modules:
  0.0 45.2 jit_solution(917678596525991400)
XLA Ops:
  0.6 41.5 %window.1 = (f32[5,1,128,512]{3,2,1,0:T(8,128)}, f32[3,256]{1,0:T(4,128)}) custom-call(f32[5,5]{1,0:T(8,128)} %coup.1, f32[3,5]{1,0:T(4,128)} %proj.1, f32[5,1,128,512]{3,2,1,0:T(8,128)} %u_hbm.1, f32[1,128,512]{2,1,0:T(8,128)} %k_hbm.1, f32[5,1,128,512]{3,2,1,0:T(8,128)} %l_hbm.1, s32[4,1,4096]{2,1,0:T(1,128)} %m_hbm.1, f32[4,1,4096]{2,1,0:T(1,128)} %w_hbm.1, ...), custom_call_target="tpu_custom_call" | custom-call | tf_op jit(solution)/shard_map/window/pallas_call | solution.py:639
  42.1 0.0 copy-start
  42.1 2.5 %copy.14 = f32[5,1,128,512]{3,2,1,0:T(8,128)} copy(f32[5,1,128,512]{3,2,1,0:T(8,128)} %get-tuple-element.4) | data formatting | bytes 2621440
  44.6 0.0 copy-done
  44.7 0.6 %copy.15 = f32[3,256]{1,0:T(4,128)} copy(f32[3,256]{1,0:T(4,128)S(1)} %copy-done) | data formatting | bytes 6144
Async XLA Ops:
  42.1 2.5 %copy-start = (f32[3,256]{1,0:T(4,128)S(1)}, f32[3,256]{1,0:T(4,128)}, u32[]{:S(2)}) copy-start(f32[3,256]{1,0:T(4,128)} %get-tuple-element.5) | copy-start | bytes 9220
